TPU v7x, 32 devices: a whole 2x2x4 slice. The times are simulated.
32 devices in a mesh: gx: 2 (over y), gy: 4 (over x, core), gz: 4 (over z).
Axes of the slice: x: 2, y: 2, z: 4, core: 2. Of those that a mesh axis runs over, the one named last changes fastest.
Arguments:
- direction: float32 [3, 32, 32, 512], P(None, 'gx', 'gy', 'gz'), may hold values from -6 to 6
- base_flow: bfloat16 [2, 3, 32, 32, 512], P(None, None, 'gx', 'gy', 'gz'), may hold values from -4 to 4
- local_inv: float32 [32, 16], P('gx'), may hold values from -1.5 to 1.5
- couple_in: float32 [4, 16], P('gx'), may hold values from -1.5 to 1.5
- couple_out: float32 [32, 2], P('gx'), may hold values from -4 to 4
- schur_inv: float32 [4, 4], replicated, may hold values from -3 to 3
- plane_x: int32 [8], replicated, may hold values from 0 to 31, as said below
- slot_plane: int32 [8], replicated, may hold values from 0 to 7, each once
- window_inv: float32 [8, 4, 4, 16, 16], P('gx', 'gy', 'gz'), may hold values from -4 to 20
Outputs:
- hess_vec: float32 [3, 32, 32, 512], P(None, 'gx', 'gy', 'gz')
Inputs may be any that keep to these rules, and one draw needn't show every extreme that they name: `plane_x`: each plane lies on a streamwise cell of the grid; the planes lie on distinct cells; at most 8 of them lie in the cells of one index d of gx (cells d*16 to d*16 + 15), and some index holds exactly 8.
All inputs are finite; a program needn't handle non-finite values.
Results may differ from a plain program's by a relative error of at most 0.0003.
Values sent between devices are 32-bit elements; how exact they have to be, the bound alone decides.
A program may use at most 64 MiB of HBM per device.

v0:
```python
import functools

import jax
import jax.numpy as jnp
from jax import lax
from jax.experimental import pallas as pl
from jax.experimental.pallas import tpu as pltpu
from jax.sharding import PartitionSpec as P

WIN = 8
time_step = 0.15
NEAR = 7.0 / 9.0
FAR = 1.0 / 36.0
C1 = 45.0 / 60.0
C2 = -9.0 / 60.0
C3 = 1.0 / 60.0
MESH = pl.DeviceIdType.MESH
high = lax.Precision.HIGHEST


def weighted(terms):
    chains = [None, None]
    for n, (coef, block) in enumerate(terms):
        part = coef * block
        chains[n % 2] = part if chains[n % 2] is None else chains[n % 2] + part
    return chains[0] if chains[1] is None else chains[0] + chains[1]


def kernel(
    sizes,
    dir_hbm, base_hbm, inv_hbm,
    local_h, in_h, out_h, schur_h, plane_h, slot_h,
    res_ref,
    dir_ref, base_ref, inv_ref, local_s, in_s, out_s, schur_s, plane_s, slot_s, in_v, near_v, near_s, esend, halo, load_sem, table_sem, ts_sem, tr_sem,
    state_one, state_two, force, acc, rhs, obs, prod_y, prod_z, hbuf,
    yside, xrecv, ysend, yrecv, zsend, zrecv, edge, winrecv, lanes_inv, blocks,
    xs_sem, xr_sem, ys_sem, yr_sem, zs_sem, zr_sem, es_sem, er_sem, ws_sem, wr_sem,
):
    n_gx, n_gy, n_gz = sizes
    gx, gy, gz = lax.axis_index("gx"), lax.axis_index("gy"), lax.axis_index("gz")
    comps, cx, cy, cz = dir_ref.shape
    wide = ysend.shape[2]
    loads = [
        pltpu.make_async_copy(src, dst, load_sem.at[n])
        for n, (src, dst) in enumerate((
            (dir_hbm, dir_ref), (in_h, in_s), (schur_h, schur_s), (local_h, local_s),
            (out_h, out_s), (plane_h, plane_s), (slot_h, slot_s),
            (base_hbm, base_ref), (inv_hbm, inv_ref), (in_h, in_v),
        ))
    ]
    owned = inv_ref.shape[0]
    y_next, y_prev = lax.rem(gy + 1, n_gy), lax.rem(gy + n_gy - 1, n_gy)
    z_next, z_prev = lax.rem(gz + 1, n_gz), lax.rem(gz + n_gz - 1, n_gz)

    @pl.when(gx == 0)
    def _():
        xrecv[:, 0] = jnp.zeros(xrecv.shape[:1] + xrecv.shape[2:], jnp.float32)

    @pl.when(gx == n_gx - 1)
    def _():
        xrecv[:, 1] = jnp.zeros(xrecv.shape[:1] + xrecv.shape[2:], jnp.float32)

    barrier = pltpu.get_barrier_semaphore()
    for d in range(1, n_gx):
        pl.semaphore_signal(barrier, device_id={"gx": lax.rem(gx + d, n_gx)}, device_id_type=MESH)
    for q in (y_prev, y_next):
        pl.semaphore_signal(barrier, device_id={"gy": q}, device_id_type=MESH)
    for q in (z_prev, z_next):
        pl.semaphore_signal(barrier, device_id={"gz": q}, device_id_type=MESH)

    for copy in loads:
        copy.start()

    def remote(src, dst, send, recv, where):
        return pltpu.make_async_remote_copy(
            src_ref=src, dst_ref=dst, send_sem=send, recv_sem=recv,
            device_id=where, device_id_type=MESH,
        )

    lane = lax.broadcasted_iota(jnp.int32, (comps, cy, cz), 2)
    sub = lax.broadcasted_iota(jnp.int32, (comps, cy, cz), 1)
    in_group = lane % WIN

    def x_copies(r, src):
        right = remote(src.at[:, cx - 2 : cx], xrecv.at[r, 0], xs_sem.at[r, 0], xr_sem.at[r, 0],
                       {"gx": lax.rem(gx + 1, n_gx)})
        left = remote(src.at[:, 0:2], xrecv.at[r, 1], xs_sem.at[r, 1], xr_sem.at[r, 1],
                      {"gx": lax.rem(gx + n_gx - 1, n_gx)})
        return right, left

    def x_start(copies):
        right, left = copies

        @pl.when(gx < n_gx - 1)
        def _():
            right.start()

        @pl.when(gx > 0)
        def _():
            left.start()

    def x_arrived(copies):
        right, left = copies

        @pl.when(gx > 0)
        def _():
            right.wait_recv()

        @pl.when(gx < n_gx - 1)
        def _():
            left.wait_recv()

    def x_sent(copies):
        right, left = copies

        @pl.when(gx < n_gx - 1)
        def _():
            right.wait_send()

        @pl.when(gx > 0)
        def _():
            left.wait_send()

    def y_copies(r):
        return (
            remote(ysend.at[r, 0], yrecv.at[r, 0], ys_sem.at[r, 0], yr_sem.at[r, 0], {"gy": y_prev}),
            remote(ysend.at[r, 1], yrecv.at[r, 1], ys_sem.at[r, 1], yr_sem.at[r, 1], {"gy": y_next}),
        )

    def z_copies(r):
        return (
            remote(zsend.at[r], zrecv.at[r, 0], zs_sem.at[r, 0], zr_sem.at[r, 0], {"gz": z_prev}),
            remote(zsend.at[r], zrecv.at[r, 1], zs_sem.at[r, 1], zr_sem.at[r, 1], {"gz": z_next}),
        )

    def edge_copies(r):
        return tuple(
            remote(edge.at[r, 0], edge.at[r, d], es_sem.at[r, d], er_sem.at[r, d],
                   {"gx": lax.rem(gx + d, n_gx)})
            for d in range(1, n_gx)
        )

    win_copies = tuple(
        remote(inv_ref, winrecv.at[d - 1], ws_sem.at[d], wr_sem.at[d], {"gx": lax.rem(gx + d, n_gx)})
        for d in range(1, n_gx)
    )

    table_copies = (
        remote(in_v, near_v.at[0], ts_sem.at[0], tr_sem.at[0], {"gx": lax.rem(gx + 1, n_gx)}),
        remote(in_v, near_v.at[1], ts_sem.at[1], tr_sem.at[1], {"gx": lax.rem(gx + n_gx - 1, n_gx)}),
    )
    left_one = jnp.where(gx > 0, 1.0, 0.0)
    right_one = jnp.where(gx < n_gx - 1, 1.0, 0.0)
    left_id, right_id = lax.rem(gx + n_gx - 1, n_gx), lax.rem(gx + 1, n_gx)

    def start(copies):
        for copy in copies:
            copy.start()

    def arrived(copies):
        for copy in copies:
            copy.wait_recv()

    def pack_y(r, src):
        lines = src.reshape(comps * cx * cy, cz)
        for c in range(comps):
            for m in range(wide):
                for side, row in ((0, m), (1, cy - wide + m)):
                    ysend[r, side, m, c] = lines[pl.ds(c * cx * cy + row, cx, stride=cy), :]

    def pack_z(r, src):
        packed = None
        for i in range(cx):
            block = src[:, i]
            turned = block if i == 0 else pltpu.roll(block, WIN * i, 2)
            if packed is None:
                packed = turned
            else:
                packed = jnp.where((lane >= WIN * i - 4) & (lane < WIN * i + 4), turned, packed)
        zsend[r] = packed

    def circular_z(block):
        def diff(k):
            return pltpu.roll(block, cz - k, 2) - pltpu.roll(block, k, 2)

        return C1 * diff(1) + C2 * diff(2) + C3 * diff(3)

    def z_fix(r):
        true = jnp.where(in_group < 4, zrecv[r, 0], zrecv[r, 1])
        delta = true - zsend[r]
        low = jnp.where(in_group >= WIN - 3, delta, 0.0)
        top = jnp.where(in_group < 3, delta, 0.0)
        low_fix = -(C1 * pltpu.roll(low, 1, 2) + C2 * pltpu.roll(low, 2, 2) + C3 * pltpu.roll(low, 3, 2))
        top_fix = (C1 * pltpu.roll(top, cz - 1, 2) + C2 * pltpu.roll(top, cz - 2, 2)
                   + C3 * pltpu.roll(top, cz - 3, 2))
        return jnp.where(in_group < 3, low_fix, 0.0) + jnp.where(in_group >= WIN - 3, top_fix, 0.0)

    def z_fix_of(fix, i):
        turned = fix if i == 0 else pltpu.roll(fix, (cz - WIN * i) % cz, 2)
        return jnp.where((lane < 3) | (lane >= cz - 3), turned, 0.0)

    def fill_sides(r):
        lines = yside.reshape(comps * cx * cy, cz)
        for c in range(comps):
            for m in range(wide):
                for side, row in ((0, m), (1, cy - wide + m)):
                    lines[pl.ds(c * cx * cy + row, cx, stride=cy), :] = yrecv[r, side, m, c]

    def along_y(block, side):
        def diff(k):
            ahead = pltpu.roll(jnp.where(sub < k, side, block), cy - k, 1)
            behind = pltpu.roll(jnp.where(sub >= cy - k, side, block), k, 1)
            return ahead - behind

        return C1 * diff(1) + C2 * diff(2) + C3 * diff(3)

    def stencil_x(src, sides, i):
        def row(n):
            if n < 0:
                return sides[0, :, n + 2]
            if n >= cx:
                return sides[1, :, n - cx]
            return src[:, n]

        return NEAR * (row(i + 1) - row(i - 1)) + FAR * (row(i + 2) - row(i - 2))

    def stencil_inside(src, i):
        total = None
        for offset, coef in ((1, NEAR), (-1, -NEAR), (2, FAR), (-2, -FAR)):
            if 0 <= i + offset < cx:
                part = coef * src[:, i + offset]
                total = part if total is None else total + part
        return total

    def velocity(n, c, i):
        return base_ref[n, c, i].astype(jnp.float32)[None]

    def fold(blocks8):
        level, m = list(blocks8), 1
        while len(level) > 1:
            keep = (lane & m) == 0
            level = [
                jnp.where(keep, a + pltpu.roll(a, cz - m, 2), b + pltpu.roll(b, m, 2))
                for a, b in zip(level[0::2], level[1::2])
            ]
            m *= 2
        return level[0]

    def unfold(block):
        level, m = [block], WIN // 2
        while m >= 1:
            keep = (lane & m) == 0
            wider = []
            for t in level:
                wider.append(jnp.where(keep, t, pltpu.roll(t, m, 2)))
                wider.append(jnp.where(keep, pltpu.roll(t, cz - m, 2), t))
            level = wider
            m //= 2
        return level

    def observe(src, dst):
        for g in range(cx // WIN):
            sums = fold([src[:, g * WIN + k] for k in range(WIN)])
            mixed = lax.dot_general(
                sums.reshape(comps * cy, cz), blocks[g], (((1,), (1,)), ((), ())),
                precision=high, preferred_element_type=jnp.float32,
            ).reshape(comps, cy, cz)
            for k, t in enumerate(unfold(mixed)):
                dst[:, g * WIN + k] = t

    def build_blocks():
        count = inv_ref.shape[2]
        spread = (
            lax.broadcasted_iota(jnp.int32, (count, cz), 1) // WIN
            == lax.broadcasted_iota(jnp.int32, (count, cz), 0)
        ).astype(jnp.float32)
        for d in range(n_gx):
            source = inv_ref[...] if d == 0 else winrecv[d - 1]
            lanes_inv[d * owned : (d + 1) * owned] = jnp.dot(
                source.reshape(owned * count, count), spread,
                precision=high, preferred_element_type=jnp.float32,
            ).reshape(owned, count, cz) * (1.0 / (WIN * WIN))
        blocks[...] = jnp.zeros(blocks.shape, jnp.float32)
        row = lax.broadcasted_iota(jnp.int32, (WIN, cz), 0)
        col = lax.broadcasted_iota(jnp.int32, (WIN, cz), 1) % WIN

        def add_slot(j, carry):
            owner = lax.rem(gx + n_gx - j // owned, n_gx)
            cell = plane_s[slot_s[owner * owned + j % owned]] - gx * cx
            for g in range(cx // WIN):
                here = (row == cell - g * WIN) & (col == cell - g * WIN)
                for s in range(count):
                    line = jnp.broadcast_to(lanes_inv[j, s : s + 1, :], (WIN, cz))
                    blocks[g, s * WIN : (s + 1) * WIN, :] += jnp.where(here, line, 0.0)
            return carry

        lax.fori_loop(0, n_gx * owned, add_slot, 0)

    def interface(r, block, m, transposed):
        terms = []
        for d in range(n_gx):
            owner = lax.rem(gx + n_gx - d, n_gx)
            for k in range(2):
                n, own = 2 * owner + k, 2 * block + m
                coef = schur_s[n, own] if transposed else schur_s[own, n]
                terms.append((coef, edge[r, d, k]))
        return weighted(terms)

    def early_copies(r):
        return tuple(
            remote(esend.at[d], edge.at[r, d], es_sem.at[r, d], er_sem.at[r, d],
                   {"gx": lax.rem(gx + d, n_gx)})
            for d in range(1, n_gx)
        )

    def early_shares(r, src):
        for i in range(cx):
            rhs[:, i] = stencil_inside(src, i)
        below = (NEAR * src[:, 0] + FAR * src[:, 1], FAR * src[:, 0])
        above = (-(NEAR * src[:, cx - 1] + FAR * src[:, cx - 2]), -FAR * src[:, cx - 1])
        parts = []
        for k in range(2):
            parts.append((2 * gx + k, weighted([(in_s[k, j], rhs[:, j]) for j in range(cx)])))
            parts.append((2 * right_id + k, right_one * (
                near_s[1, k, 0] * above[0] + near_s[1, k, 1] * above[1])))
            parts.append((2 * left_id + k, left_one * (
                near_s[0, k, cx - 1] * below[0] + near_s[0, k, cx - 2] * below[1])))
        for d in tuple(range(1, n_gx)) + (0,):
            owner = lax.rem(gx + d, n_gx)
            for m in range(2):
                share = weighted([(schur_s[2 * owner + m, n], part) for n, part in parts])
                if d == 0:
                    edge[r, 0, m] = share
                else:
                    esend[d, m] = share

    sent = []

    def tangent(r, n, src, dst, first, shadow):
        xc, yc, zc = x_copies(r, src), y_copies(r), z_copies(r)
        ec = edge_copies(r) if first else early_copies(r)
        if first:
            loads[0].wait()
        else:
            x_start(xc)
        pack_z(r, src)
        if not first:
            start(zc)
        pack_y(r, src)
        if first:
            pl.semaphore_wait(barrier, n_gx - 1 + 4)
            x_start(xc)
            start(zc)
        start(yc)
        if not first:
            early_shares(r, src)
            start(ec)
        sent.append((xc, yc + zc + ec))
        if first:
            for copy in loads[1:]:
                copy.wait()
            start(table_copies)
        for i in range(cx):
            block = src[:, i]
            acc[:, i] = block - time_step * (velocity(n, 2, i) * circular_z(block))
        x_arrived(xc)
        for i in range(cx) if first else (0, 1, cx - 2, cx - 1):
            rhs[:, i] = stencil_x(src, xrecv.at[r], i)
        if first:
            for k in range(2):
                edge[r, 0, k] = weighted([(in_s[k, j], rhs[:, j]) for j in range(cx)])
            start(ec)
            start(win_copies)
        for i in range(cx):
            solved = weighted([(local_s[i, j], rhs[:, j]) for j in range(cx)])
            acc[:, i] -= time_step * (velocity(n, 0, i) * solved)
        if first:
            arrived(table_copies)
            table = pltpu.make_async_copy(near_v, near_s, table_sem.at[0])
            table.start()
            table.wait()
        shadow()
        arrived(yc)
        fill_sides(r)
        for i in range(cx):
            acc[:, i] -= time_step * (velocity(n, 1, i) * along_y(src[:, i], yside[:, i]))
        arrived(zc)
        fix = z_fix(r)
        arrived(ec)
        if first:
            values = [interface(r, gx, m, False) for m in range(2)]
        else:
            values = [weighted([(1.0, edge[r, d, m]) for d in range(n_gx)]) for m in range(2)]
        for i in range(cx):
            pulled = out_s[0, i] * values[0] + out_s[1, i] * values[1]
            dst[:, i] = acc[:, i] - time_step * (
                velocity(n, 0, i) * pulled + velocity(n, 2, i) * z_fix_of(fix, i)
            )

    def adjoint(r, n, src, dst, extra):
        xc, yc, zc, ec = x_copies(r, hbuf.at[r - 2]), y_copies(r), z_copies(r), edge_copies(r)
        sent.append((xc, yc + zc + ec))
        held = hbuf.at[r - 2]
        for i in range(cx):
            prod_z[:, i] = velocity(n, 2, i) * src[:, i]
        pack_z(r, prod_z)
        start(zc)
        for i in range(cx):
            prod_y[:, i] = velocity(n, 1, i) * src[:, i]
        pack_y(r, prod_y)
        start(yc)
        for i in range(cx):
            rhs[:, i] = velocity(n, 0, i) * src[:, i]
        for k in range(2):
            edge[r, 0, k] = weighted([(out_s[k, i], rhs[:, i]) for i in range(cx)])
        start(ec)
        order = (0, 1, cx - 2, cx - 1) + tuple(range(2, cx - 2))
        for place, i in enumerate(order):
            held[:, i] = weighted([(local_s[j, i], rhs[:, j]) for j in range(cx)])
            if place == 3:
                x_start(xc)
        for i in range(cx):
            total = src[:, i] + time_step * circular_z(prod_z[:, i])
            acc[:, i] = total if extra is None else total + extra[:, i]
        arrived(ec)
        values = [interface(r, gx, m, True) for m in range(2)]
        lower = [left_one * interface(r, left_id, m, True) for m in range(2)]
        upper = [right_one * interface(r, right_id, m, True) for m in range(2)]
        for i in range(cx):
            rhs[:, i] = held[:, i] + (in_s[0, i] * values[0] + in_s[1, i] * values[1])
        for i in range(2, cx - 2):
            acc[:, i] += time_step * stencil_x(rhs, halo, i)
        x_arrived(xc)
        for n in range(2):
            halo[0, :, n] = xrecv[r, 0, :, n] + (
                near_s[0, 0, cx - 2 + n] * lower[0] + near_s[0, 1, cx - 2 + n] * lower[1])
            halo[1, :, n] = xrecv[r, 1, :, n] + (
                near_s[1, 0, n] * upper[0] + near_s[1, 1, n] * upper[1])
        for i in (0, 1, cx - 2, cx - 1):
            acc[:, i] += time_step * stencil_x(rhs, halo, i)
        arrived(yc)
        fill_sides(r)
        for i in range(cx):
            acc[:, i] += time_step * along_y(prod_y[:, i], yside[:, i])
        arrived(zc)
        fix = z_fix(r)
        for i in range(cx):
            dst[:, i] = acc[:, i] + time_step * z_fix_of(fix, i)

    def nothing():
        pass

    def observe_one():
        arrived(win_copies)
        build_blocks()
        observe(state_one, obs)

    tangent(0, 0, dir_ref, state_one, True, nothing)
    tangent(1, 1, state_one, state_two, False, observe_one)
    observe(state_two, force)
    adjoint(2, 1, force, state_two, obs)
    adjoint(3, 0, state_two, res_ref, None)
    for xc, rest in sent:
        x_sent(xc)
        for copy in rest:
            copy.wait_send()
    for copy in win_copies + table_copies:
        copy.wait_send()


def solution(mesh):
    sizes = tuple(mesh.shape[name] for name in ("gx", "gy", "gz"))

    def local(direction, base_flow, local_inv, couple_in, couple_out, schur_inv,
              plane_x, slot_plane, window_inv):
        n_gx = sizes[0]
        comps, cx, cy, cz = direction.shape
        owned, count = window_inv.shape[0], window_inv.shape[3]
        wide = 3
        field = pltpu.VMEM(direction.shape, jnp.float32)

        def held(*shape):
            return pltpu.VMEM(shape, jnp.float32)

        sems = pltpu.SemaphoreType.DMA
        vmem = pl.BlockSpec(memory_space=pltpu.VMEM)
        kept = functools.partial(pltpu.with_memory_space_constraint, memory_space=pltpu.HBM)
        hbm = pl.BlockSpec(memory_space=pltpu.HBM)
        tables = (local_inv, couple_in, couple_out.T, schur_inv, plane_x, slot_plane)
        pulled = pl.pallas_call(
            functools.partial(kernel, sizes),
            out_shape=jax.ShapeDtypeStruct(direction.shape, jnp.float32),
            in_specs=[hbm] * 9,
            out_specs=vmem,
            scratch_shapes=[
                field, pltpu.VMEM(base_flow.shape, base_flow.dtype), held(owned, count, count),
            ] + [pltpu.SMEM(t.shape, t.dtype) for t in tables] + [
                held(2, cx), held(2, 2, cx), pltpu.SMEM((2, 2, cx), jnp.float32),
                held(n_gx, 2, comps, cy, cz), held(2, comps, 2, cy, cz),
                sems((10,)), sems((1,)), sems((2,)), sems((2,)),
            ] + [field] * 8 + [
                held(2, comps, cx, cy, cz),
                field,
                held(4, 2, comps, 2, cy, cz),
                held(4, 2, wide, comps, cx, cz),
                held(4, 2, wide, comps, cx, cz),
                held(4, comps, cy, cz),
                held(4, 2, comps, cy, cz),
                held(4, n_gx, 2, comps, cy, cz),
                held(n_gx - 1, owned, count, count),
                held(n_gx * owned, count, cz),
                held(cx // WIN, count * WIN, cz),
                sems((4, 2)), sems((4, 2)), sems((4, 2)), sems((4, 2)), sems((4, 2)), sems((4, 2)),
                sems((4, n_gx)), sems((4, n_gx)), sems((n_gx,)), sems((n_gx,)),
            ],
            compiler_params=pltpu.CompilerParams(collective_id=0, has_side_effects=True, vmem_limit_bytes=16 * 2**20),
        )(
            *map(kept, (direction, base_flow, window_inv.reshape(owned, count, count)) + tables),
        )
        return pulled + direction

    return jax.shard_map(
        local,
        mesh=mesh,
        in_specs=(
            P(None, "gx", "gy", "gz"),
            P(None, None, "gx", "gy", "gz"),
            P("gx", None),
            P("gx", None),
            P("gx", None),
            P(),
            P(),
            P(),
            P("gx", "gy", "gz", None, None),
        ),
        out_specs=P(None, "gx", "gy", "gz"),
        check_vma=False,
    )
```

profile of v0, /device:TPU:0, one launch (start us, length us, event | category | flops | bytes accessed | tf_op | source)
XLA Modules:
  0.0 26.4 jit_solution(11240678789099837477)
XLA Ops:
  0.0 0.0 copy-start
  0.0 25.7 %shard_map.91 = f32[3,16,8,128]{3,2,1,0:T(8,128)S(1)} custom-call(f32[3,16,8,128]{3,2,1,0:T(8,128)} %dir_hbm.1, bf16[2,3,16,8,128]{4,3,2,1,0:T(8,128)(2,1)} %base_hbm.1, f32[4,16,16]{2,1,0:T(8,128)} %bitcast.2, f32[16,16]{1,0:T(8,128)} %local_h.1, f32[2,16]{1,0:T(2,128)} %in_h.1, f32[2,16]{1,0:T(2,128)} %bitcast.3, f32[4,4]{1,0:T(4,128)} %schur_h.1, ...), custom_call_target="tpu_custom_call" | custom-call | tf_op jit(solution)/shard_map/pallas_call | solution.py:490
  25.7 0.0 copy-done
  25.7 0.7 %add.3 = f32[3,16,8,128]{3,2,1,0:T(8,128)} add(f32[3,16,8,128]{3,2,1,0:T(8,128)S(1)} %shard_map.91, f32[3,16,8,128]{3,2,1,0:T(8,128)S(1)} %copy-done) | non-fusion elementwise | flops 49152 | bytes 589824 | tf_op jit(solution)/shard_map/add | solution.py:520
Async XLA Ops:
  0.0 25.7 %copy-start = (f32[3,16,8,128]{3,2,1,0:T(8,128)S(1)}, f32[3,16,8,128]{3,2,1,0:T(8,128)}, u32[]{:S(2)}) copy-start(f32[3,16,8,128]{3,2,1,0:T(8,128)} %dir_hbm.1) | copy-start | bytes 589828
where the time goes:
time: 26.6 us; the launch traced here: 26.4 us
  Pallas kernels  25.7 us (97%)
  other arithmetic  0.7 us (3%)
    pallas_call x1, Pallas kernels, local(): pl.pallas_call(functools.partial(kernel, sizes), out_shape=jax.ShapeDtype...  25.7 us
    add x1, other arithmetic, local(): return pulled + direction  0.7 us

commit v1 on v0

--- a/solution.py
+++ b/solution.py
@@ -468,6 +468,382 @@
         copy.wait_send()
 
 
+def pair_kernel(
+    sizes,
+    dir_hbm, base_hbm, inv_hbm,
+    local_h, in_h, out_h, schur_h, plane_h, slot_h,
+    res_ref,
+    dir_ref, base_ref, inv_ref, local_s, in_s, out_s, schur_s, plane_s, slot_s, in_v, near_v, near_s,
+    state_one, state_two, force, acc, rhs, obs, prod, held, yside, vel, uz_pack,
+    xsend, xrecv, ysend, yrecv, zsend, zrecv, winrecv, lanes_inv, blocks,
+    load_sem, side_sem, xs_sem, xr_sem, ys_sem, yr_sem, zs_sem, zr_sem,
+):
+    n_gx, n_gy, n_gz = sizes
+    gx, gy, gz = lax.axis_index("gx"), lax.axis_index("gy"), lax.axis_index("gz")
+    comps, cx, cy, cz = dir_ref.shape
+    wide = ysend.shape[2]
+    owned = inv_ref.shape[0]
+    other = 1 - gx
+    y_next, y_prev = lax.rem(gy + 1, n_gy), lax.rem(gy + n_gy - 1, n_gy)
+    z_next, z_prev = lax.rem(gz + 1, n_gz), lax.rem(gz + n_gz - 1, n_gz)
+    first = gx == 0
+    near_row = jnp.where(first, cx - 2, 0)
+    their_row = jnp.where(first, 0, cx - 2)
+
+    barrier = pltpu.get_barrier_semaphore()
+    for q in (z_prev, z_next):
+        pl.semaphore_signal(barrier, device_id={"gz": q}, device_id_type=MESH)
+    pl.semaphore_signal(barrier, device_id={"gx": other}, device_id_type=MESH)
+    for q in (y_prev, y_next):
+        pl.semaphore_signal(barrier, device_id={"gy": q}, device_id_type=MESH)
+
+    loads = [
+        pltpu.make_async_copy(src, dst, load_sem.at[n])
+        for n, (src, dst) in enumerate((
+            (dir_hbm, dir_ref), (in_h, in_s), (in_h, in_v), (base_hbm, base_ref), (local_h, local_s),
+            (schur_h, schur_s), (out_h, out_s), (plane_h, plane_s), (slot_h, slot_s), (inv_hbm, inv_ref),
+        ))
+    ]
+    for copy in loads:
+        copy.start()
+
+    def remote(src, dst, send, recv, where):
+        return pltpu.make_async_remote_copy(
+            src_ref=src, dst_ref=dst, send_sem=send, recv_sem=recv,
+            device_id=where, device_id_type=MESH,
+        )
+
+    def x_copy(r):
+        return remote(xsend.at[r], xrecv.at[r], xs_sem.at[r % 2], xr_sem.at[r % 2], {"gx": other})
+
+    def y_copies(r):
+        return tuple(
+            remote(ysend.at[r, d], yrecv.at[r, d], ys_sem.at[r % 2], yr_sem.at[r % 2], {"gy": q})
+            for d, q in enumerate((y_prev, y_next))
+        )
+
+    def z_copies(r):
+        return tuple(
+            remote(zsend.at[r], zrecv.at[r, d], zs_sem.at[r % 2], zr_sem.at[r % 2], {"gz": q})
+            for d, q in enumerate((z_prev, z_next))
+        )
+
+    def y_both(r):
+        return remote(yrecv.at[r], yrecv.at[r], ys_sem.at[r % 2], yr_sem.at[r % 2], {"gy": y_next})
+
+    def z_both(r):
+        return remote(zrecv.at[r], zrecv.at[r], zs_sem.at[r % 2], zr_sem.at[r % 2], {"gz": z_next})
+
+    def settle(r):
+        if r >= 0:
+            x_copy(r).wait_send()
+            y_both(r).wait_send()
+            z_both(r).wait_send()
+
+    win_copy = remote(inv_ref, winrecv, side_sem.at[0], side_sem.at[1], {"gx": other})
+    table_copy = remote(in_v, near_v, side_sem.at[2], side_sem.at[3], {"gx": other})
+
+    lane = lax.broadcasted_iota(jnp.int32, (cy, cz), 1)
+    in_group = lane % WIN
+    cell_of = ((lane + WIN // 2) // WIN) % cx
+    near_edge = (lane < 3) | (lane >= cz - 3)
+    left, right = in_group < 3, in_group >= WIN - 3
+    ahead = in_group < WIN // 2
+
+    def packed(block_of):
+        total = None
+        for i in range(cx):
+            block = block_of(i)
+            turned = block if i == 0 else pltpu.roll(block, WIN * i, block.ndim - 1)
+            total = turned if total is None else jnp.where(cell_of == i, turned, total)
+        return total
+
+    def unpacked(block, i):
+        turned = block if i == 0 else pltpu.roll(block, (cz - WIN * i) % cz, 2)
+        return jnp.where(near_edge, turned, 0.0)
+
+    def pack_y(r, src):
+        lines = src.reshape(comps * cx * cy, cz)
+        for side, start in ((0, 0), (1, cy - wide)):
+            for m in range(wide):
+                for c in range(comps):
+                    ysend[r, side, m, c] = lines[pl.ds(c * cx * cy + start + m, cx, stride=cy), :]
+
+    def circular(block, axis):
+        size = block.shape[axis]
+
+        def diff(k):
+            return pltpu.roll(block, size - k, axis) - pltpu.roll(block, k, axis)
+
+        return C1 * diff(1) + C2 * diff(2) + C3 * diff(3)
+
+    def z_fix(r):
+        delta = jnp.where(ahead, zrecv[r, 0], zrecv[r, 1]) - zsend[r]
+        low = jnp.where(right, delta, 0.0)
+        top = jnp.where(left, delta, 0.0)
+        low_fix = -(C1 * pltpu.roll(low, 1, 2) + C2 * pltpu.roll(low, 2, 2) + C3 * pltpu.roll(low, 3, 2))
+        top_fix = (C1 * pltpu.roll(top, cz - 1, 2) + C2 * pltpu.roll(top, cz - 2, 2)
+                   + C3 * pltpu.roll(top, cz - 3, 2))
+        return jnp.where(left, low_fix, jnp.where(right, top_fix, 0.0))
+
+    def y_fix(r):
+        lines = yside.reshape(comps * cx * cy, cz)
+        for c in range(comps):
+            def put(row, value):
+                lines[pl.ds(c * cx * cy + row, cx, stride=cy), :] = value
+
+            d0, d1, d2 = (yrecv[r, 0, m, c] - ysend[r, 0, m, c] for m in range(3))
+            put(cy - 1, C1 * d0 + C2 * d1 + C3 * d2)
+            put(cy - 2, C2 * d0 + C3 * d1)
+            put(cy - 3, C3 * d0)
+            d0, d1, d2 = (yrecv[r, 1, m, c] - ysend[r, 1, m, c] for m in range(3))
+            put(0, -(C1 * d2 + C2 * d1 + C3 * d0))
+            put(1, -(C2 * d2 + C3 * d1))
+            put(2, -(C3 * d2))
+
+    def stencil_inside(row, i):
+        total = None
+        for step, coef in ((1, NEAR), (2, FAR)):
+            up, down = i + step < cx, i - step >= 0
+            if up and down:
+                part = coef * (row(i + step) - row(i - step))
+            elif up:
+                part = coef * row(i + step)
+            elif down:
+                part = -coef * row(i - step)
+            else:
+                continue
+            total = part if total is None else total + part
+        return total
+
+    def rows_of(ref):
+        return lambda i: ref[:, i]
+
+    def across(pair, to_first):
+        low, high = pair
+        upper = (FAR * low, NEAR * low + FAR * high)
+        lower = (-(NEAR * high + FAR * low), -FAR * high)
+        return tuple(jnp.where(to_first, u, d) for u, d in zip(upper, lower))
+
+    def fold(blocks8):
+        level, m = list(blocks8), 1
+        while len(level) > 1:
+            keep = (lane & m) == 0
+            level = [
+                jnp.where(keep, a + pltpu.roll(a, cz - m, 2), b + pltpu.roll(b, m, 2))
+                for a, b in zip(level[0::2], level[1::2])
+            ]
+            m *= 2
+        return level[0]
+
+    def unfold(block):
+        level, m = [block], WIN // 2
+        while m >= 1:
+            keep = (lane & m) == 0
+            wider = []
+            for t in level:
+                wider.append(jnp.where(keep, t, pltpu.roll(t, m, 2)))
+                wider.append(jnp.where(keep, pltpu.roll(t, cz - m, 2), t))
+            level = wider
+            m //= 2
+        return level
+
+    def observe(src, dst):
+        for g in range(cx // WIN):
+            sums = fold([src[:, g * WIN + k] for k in range(WIN)])
+            mixed = lax.dot_general(
+                sums.reshape(comps * cy, cz), blocks[g], (((1,), (1,)), ((), ())),
+                precision=high, preferred_element_type=jnp.float32,
+            ).reshape(comps, cy, cz)
+            for k, t in enumerate(unfold(mixed)):
+                dst[:, g * WIN + k] = t
+
+    def build_blocks():
+        count = inv_ref.shape[2]
+        spread = (
+            lax.broadcasted_iota(jnp.int32, (count, cz), 1) // WIN
+            == lax.broadcasted_iota(jnp.int32, (count, cz), 0)
+        ).astype(jnp.float32)
+        for d, source in enumerate((inv_ref, winrecv)):
+            lanes_inv[d * owned : (d + 1) * owned] = jnp.dot(
+                source[...].reshape(owned * count, count), spread,
+                precision=high, preferred_element_type=jnp.float32,
+            ).reshape(owned, count, cz) * (1.0 / (WIN * WIN))
+        blocks[...] = jnp.zeros(blocks.shape, jnp.float32)
+        row = lax.broadcasted_iota(jnp.int32, (WIN, cz), 0)
+        col = lax.broadcasted_iota(jnp.int32, (WIN, cz), 1) % WIN
+
+        def add_slot(j, carry):
+            owner = jnp.where(j < owned, gx, other)
+            cell = plane_s[slot_s[owner * owned + j % owned]] - gx * cx
+            for g in range(cx // WIN):
+                here = (row == cell - g * WIN) & (col == cell - g * WIN)
+                for s in range(count):
+                    line = jnp.broadcast_to(lanes_inv[j, s : s + 1, :], (WIN, cz))
+                    blocks[g, s * WIN : (s + 1) * WIN, :] += jnp.where(here, line, 0.0)
+            return carry
+
+        lax.fori_loop(0, n_gx * owned, add_slot, 0)
+
+    def start(copies):
+        for copy in copies:
+            copy.start()
+
+    def tangent(r, n, src, dst, edge, shadow):
+        settle(r - 2)
+        zsend[r] = edge
+        if r:
+            start(z_copies(r))
+        pack_y(r, src)
+        if not r:
+            pl.semaphore_wait(barrier, n_gx - 1 + 4)
+            start(z_copies(r))
+        start(y_copies(r))
+        ours = src[:, pl.ds(near_row, 2)]
+        for k in range(2):
+            xsend[r, k] = ours[:, k]
+        if not r:
+            loads[2].wait()
+            table_copy.start()
+            loads[1].wait()
+        for i in range(cx):
+            rhs[:, i] = stencil_inside(rows_of(src), i)
+        for k in range(2):
+            xsend[r, 2 + k] = weighted([(in_s[k, j], rhs[:, j]) for j in range(cx)])
+        x_copy(r).start()
+        if not r:
+            for copy in loads[3:]:
+                copy.wait()
+            win_copy.start()
+            for m in range(2):
+                for c in range(comps):
+                    for i in range(cx):
+                        vel[m, c, i] = time_step * base_ref[m, c, i].astype(jnp.float32)
+                uz_pack[m] = packed(lambda i: vel[m, 2, i])
+            yside[...] = jnp.zeros(yside.shape, jnp.float32)
+        for i in range(cx):
+            block = src[:, i]
+            solved = weighted([(local_s[i, j], rhs[:, j]) for j in range(cx)])
+            acc[:, i] = block - (
+                vel[n, 2, i] * circular(block, 2) + vel[n, 1, i] * circular(block, 1) + vel[n, 0, i] * solved)
+        shadow()
+        x_copy(r).wait_recv()
+        pair = xrecv[r, 0], xrecv[r, 1]
+        halo = across(pair, first)
+        own = [
+            xsend[r, 2 + k] + in_s[k, near_row] * halo[0] + in_s[k, near_row + 1] * halo[1] for k in range(2)
+        ]
+        away = across((xsend[r, 0], xsend[r, 1]), gx != 0)
+        theirs = [
+            xrecv[r, 2 + k] + near_s[k, their_row] * away[0] + near_s[k, their_row + 1] * away[1]
+            for k in range(2)
+        ]
+        values = [
+            weighted([(schur_s[2 * gx + m, 2 * gx + k], own[k]) for k in range(2)]
+                     + [(schur_s[2 * gx + m, 2 * other + k], theirs[k]) for k in range(2)])
+            for m in range(2)
+        ]
+        for i in range(cx):
+            acc[:, i] -= vel[n, 0, i] * weighted([
+                (local_s[i, near_row], halo[0]), (local_s[i, near_row + 1], halo[1]),
+                (out_s[0, i], values[0]), (out_s[1, i], values[1])])
+        y_both(r).wait_recv()
+        y_fix(r)
+        for i in range(cx):
+            acc[:, i] -= vel[n, 1, i] * yside[:, i]
+        before = packed(rows_of(acc))
+        z_both(r).wait_recv()
+        fix = uz_pack[n] * z_fix(r)
+        after = before - fix
+
+        def finish():
+            for i in range(cx):
+                dst[:, i] = acc[:, i] - unpacked(fix, i)
+
+        return after, finish
+
+    def adjoint(r, n, src, dst, edge, finish_src, extra):
+        settle(r - 2)
+        zsend[r] = uz_pack[n] * edge
+        start(z_copies(r))
+        finish_src()
+        for i in range(cx):
+            prod[:, i] = vel[n, 1, i] * src[:, i]
+        pack_y(r, prod)
+        start(y_copies(r))
+        for i in range(cx):
+            rhs[:, i] = vel[n, 0, i] * src[:, i]
+        for k in range(2):
+            xsend[r, k] = weighted([(local_s[j, near_row + k], rhs[:, j]) for j in range(cx)])
+            xsend[r, 2 + k] = weighted([(out_s[k, j], rhs[:, j]) for j in range(cx)])
+        x_copy(r).start()
+        for i in range(cx):
+            held[:, i] = weighted([(local_s[j, i], rhs[:, j]) for j in range(cx)])
+        for i in range(cx):
+            total = src[:, i] + circular(vel[n, 2, i] * src[:, i], 2) + circular(prod[:, i], 1)
+            if extra is not None:
+                total = total + extra[:, i]
+            acc[:, i] = total + stencil_inside(rows_of(held), i)
+        x_copy(r).wait_recv()
+
+        def solved(block):
+            return [
+                weighted([(schur_s[2 * gx + k, 2 * block + m], xsend[r, 2 + k]) for k in range(2)]
+                         + [(schur_s[2 * other + k, 2 * block + m], xrecv[r, 2 + k]) for k in range(2)])
+                for m in range(2)
+            ]
+
+        own, theirs = solved(gx), solved(other)
+        halo = across([
+            xrecv[r, k] + near_s[0, their_row + k] * theirs[0] + near_s[1, their_row + k] * theirs[1]
+            for k in range(2)
+        ], first)
+        for i in range(cx):
+            acc[:, i] += weighted([
+                (stencil_inside(lambda j, m=m: in_s[m, j], i), own[m]) for m in range(2)])
+        for k in range(2):
+            acc[:, near_row + k] += halo[k]
+        y_both(r).wait_recv()
+        y_fix(r)
+        for i in range(cx):
+            acc[:, i] += yside[:, i]
+        before = packed(rows_of(acc))
+        z_both(r).wait_recv()
+        fix = z_fix(r)
+        after = before + fix
+
+        def finish():
+            for i in range(cx):
+                dst[:, i] = acc[:, i] + unpacked(fix, i)
+
+        return after, finish
+
+    def table():
+        table_copy.wait_recv()
+        copy = pltpu.make_async_copy(near_v, near_s, load_sem.at[0])
+        copy.start()
+        copy.wait()
+
+    def observe_one():
+        win_copy.wait_recv()
+        build_blocks()
+        observe(state_one, obs)
+
+    loads[0].wait()
+    edge, finish = tangent(0, 0, dir_ref, state_one, packed(rows_of(dir_ref)), table)
+    finish()
+    edge, finish = tangent(1, 1, state_one, state_two, edge, observe_one)
+    finish()
+    observe(state_two, force)
+    edge, finish = adjoint(2, 1, force, state_two, packed(rows_of(force)), lambda: None, obs)
+    edge, finish = adjoint(3, 0, state_two, res_ref, edge, finish, None)
+    finish()
+    settle(2)
+    settle(3)
+    win_copy.wait_send()
+    table_copy.wait_send()
+
+
 def solution(mesh):
     sizes = tuple(mesh.shape[name] for name in ("gx", "gy", "gz"))
 
@@ -487,14 +863,35 @@
         kept = functools.partial(pltpu.with_memory_space_constraint, memory_space=pltpu.HBM)
         hbm = pl.BlockSpec(memory_space=pltpu.HBM)
         tables = (local_inv, couple_in, couple_out.T, schur_inv, plane_x, slot_plane)
-        pulled = pl.pallas_call(
-            functools.partial(kernel, sizes),
+        operands = tuple(map(kept, (direction, base_flow, window_inv.reshape(owned, count, count)) + tables))
+        call = functools.partial(
+            pl.pallas_call,
             out_shape=jax.ShapeDtypeStruct(direction.shape, jnp.float32),
             in_specs=[hbm] * 9,
             out_specs=vmem,
-            scratch_shapes=[
-                field, pltpu.VMEM(base_flow.shape, base_flow.dtype), held(owned, count, count),
-            ] + [pltpu.SMEM(t.shape, t.dtype) for t in tables] + [
+            compiler_params=pltpu.CompilerParams(collective_id=0, has_side_effects=True, vmem_limit_bytes=16 * 2**20),
+        )
+        loaded = [
+            field, pltpu.VMEM(base_flow.shape, base_flow.dtype), held(owned, count, count),
+        ] + [pltpu.SMEM(t.shape, t.dtype) for t in tables]
+        if n_gx == 2:
+            pulled = call(
+                functools.partial(pair_kernel, sizes),
+                scratch_shapes=loaded + [
+                    held(2, cx), held(2, cx), pltpu.SMEM((2, cx), jnp.float32),
+                ] + [field] * 9 + [
+                    held(*base_flow.shape), held(2, cy, cz),
+                    held(4, 4, comps, cy, cz), held(4, 4, comps, cy, cz),
+                    held(4, 2, wide, comps, cx, cz), held(4, 2, wide, comps, cx, cz),
+                    held(4, comps, cy, cz), held(4, 2, comps, cy, cz),
+                    held(owned, count, count), held(n_gx * owned, count, cz), held(cx // WIN, count * WIN, cz),
+                    sems((10,)), sems((4,)),
+                ] + [sems((2,))] * 6,
+            )(*operands)
+            return pulled + direction
+        pulled = call(
+            functools.partial(kernel, sizes),
+            scratch_shapes=loaded + [
                 held(2, cx), held(2, 2, cx), pltpu.SMEM((2, 2, cx), jnp.float32),
                 held(n_gx, 2, comps, cy, cz), held(2, comps, 2, cy, cz),
                 sems((10,)), sems((1,)), sems((2,)), sems((2,)),
@@ -513,10 +910,7 @@
                 sems((4, 2)), sems((4, 2)), sems((4, 2)), sems((4, 2)), sems((4, 2)), sems((4, 2)),
                 sems((4, n_gx)), sems((4, n_gx)), sems((n_gx,)), sems((n_gx,)),
             ],
-            compiler_params=pltpu.CompilerParams(collective_id=0, has_side_effects=True, vmem_limit_bytes=16 * 2**20),
-        )(
-            *map(kept, (direction, base_flow, window_inv.reshape(owned, count, count)) + tables),
-        )
+        )(*operands)
         return pulled + direction
 
     return jax.shard_map(

time: 26.6 us -> 22.6 us (0.85)
  Pallas kernels: 25.7 us -> 21.7 us
    pallas_call x1, Pallas kernels: 25.7 us -> 21.7 us  [local(): call(functools.partial(pair_kernel, sizes), scratch_shapes=loaded + [held...]
where the time goes in v1:
time: 22.6 us; the launch traced here: 22.4 us
  Pallas kernels  21.7 us (96%)
  other arithmetic  0.7 us (3%)
    pallas_call x1, Pallas kernels, local(): call(functools.partial(pair_kernel, sizes), scratch_shapes=loaded + [held...  21.7 us
    add x1, other arithmetic, local(): return pulled + direction  0.7 us

profile of v1, /device:TPU:0, one launch (start us, length us, event | category | flops | bytes accessed | tf_op | source)
XLA Modules:
  0.0 22.4 jit_solution(2551903575564784006)
XLA Ops:
  0.0 0.0 copy-start
  0.0 21.7 %shard_map.91 = f32[3,16,8,128]{3,2,1,0:T(8,128)S(1)} custom-call(f32[3,16,8,128]{3,2,1,0:T(8,128)} %dir_hbm.1, bf16[2,3,16,8,128]{4,3,2,1,0:T(8,128)(2,1)} %base_hbm.1, f32[4,16,16]{2,1,0:T(8,128)} %bitcast.2, f32[16,16]{1,0:T(8,128)} %local_h.1, f32[2,16]{1,0:T(2,128)} %in_h.1, f32[2,16]{1,0:T(2,128)} %bitcast.3, f32[4,4]{1,0:T(4,128)} %schur_h.1, ...), custom_call_target="tpu_custom_call" | custom-call | tf_op jit(solution)/shard_map/pallas_call | solution.py:878
  21.7 0.0 copy-done
  21.7 0.7 %add.3 = f32[3,16,8,128]{3,2,1,0:T(8,128)} add(f32[3,16,8,128]{3,2,1,0:T(8,128)S(1)} %shard_map.91, f32[3,16,8,128]{3,2,1,0:T(8,128)S(1)} %copy-done) | non-fusion elementwise | flops 49152 | bytes 589824 | tf_op jit(solution)/shard_map/add | solution.py:891
Async XLA Ops:
  0.0 21.7 %copy-start = (f32[3,16,8,128]{3,2,1,0:T(8,128)S(1)}, f32[3,16,8,128]{3,2,1,0:T(8,128)}, u32[]{:S(2)}) copy-start(f32[3,16,8,128]{3,2,1,0:T(8,128)} %dir_hbm.1) | copy-start | bytes 589828

commit v2 on v1

--- a/solution.py
+++ b/solution.py
@@ -474,8 +474,8 @@
     local_h, in_h, out_h, schur_h, plane_h, slot_h,
     res_ref,
     dir_ref, base_ref, inv_ref, local_s, in_s, out_s, schur_s, plane_s, slot_s, in_v, near_v, near_s,
-    state_one, state_two, force, acc, rhs, obs, prod, held, yside, vel, uz_pack,
-    xsend, xrecv, ysend, yrecv, zsend, zrecv, winrecv, lanes_inv, blocks,
+    state_one, costate, force, acc, rhs, obs, prod, held, yside, vel, uz_pack,
+    xsend, xrecv, ysend, yrecv, zsend, zrecv, winrecv, lanes_inv, blocks, seen_w, fix_rows, fix_edge, mixed,
     load_sem, side_sem, xs_sem, xr_sem, ys_sem, yr_sem, zs_sem, zr_sem,
 ):
     n_gx, n_gy, n_gz = sizes
@@ -648,14 +648,46 @@
             m //= 2
         return level
 
+    def product(a, b, side):
+        return lax.dot_general(
+            a, b, (((1,), (side,)), ((), ())), precision=high, preferred_element_type=jnp.float32)
+
+    def parts(a):
+        high_part = a.astype(jnp.bfloat16)
+        return high_part, (a - high_part.astype(jnp.float32)).astype(jnp.bfloat16)
+
+    def weights(a):
+        one, two = parts(a)
+        return jnp.concatenate([one, two, one], axis=0)
+
+    def apply(a, stacked):
+        one, two = parts(a)
+        return jnp.dot(
+            jnp.concatenate([one, one, two], axis=1), stacked, preferred_element_type=jnp.float32)
+
+    def build_edges():
+        count = inv_ref.shape[2]
+        place = lax.broadcasted_iota(jnp.int32, (cz, cz), 0)
+        column = lax.broadcasted_iota(jnp.int32, (cz, cz), 1)
+        cell = ((place + WIN // 2) // WIN) % cx
+        target = cell % WIN + jnp.where(place % WIN < WIN // 2, 0, (count - 1) * WIN)
+        total = None
+        for g in range(cx // WIN):
+            chosen = ((cell // WIN == g) & (column == target)).astype(jnp.float32)
+            turned = blocks[g].T
+            onto_edge = product(turned, chosen, 1)
+            seen_w[g, :, :cz] = weights(turned)
+            seen_w[g, :, cz:] = weights(onto_edge)
+            fix_rows[g] = weights(product(chosen, turned, 0))
+            part = product(chosen, onto_edge, 0)
+            total = part if total is None else total + part
+        fix_edge[...] = weights(total)
+
     def observe(src, dst):
         for g in range(cx // WIN):
             sums = fold([src[:, g * WIN + k] for k in range(WIN)])
-            mixed = lax.dot_general(
-                sums.reshape(comps * cy, cz), blocks[g], (((1,), (1,)), ((), ())),
-                precision=high, preferred_element_type=jnp.float32,
-            ).reshape(comps, cy, cz)
-            for k, t in enumerate(unfold(mixed)):
+            total = apply(sums.reshape(comps * cy, cz), seen_w[g, :, :cz]).reshape(comps, cy, cz)
+            for k, t in enumerate(unfold(total)):
                 dst[:, g * WIN + k] = t
 
     def build_blocks():
@@ -689,15 +721,13 @@
         for copy in copies:
             copy.start()
 
-    def tangent(r, n, src, dst, edge, shadow):
-        settle(r - 2)
+    def tangent(r, n, src, edge, finish_src, shadow, close):
         zsend[r] = edge
-        if r:
-            start(z_copies(r))
-        pack_y(r, src)
         if not r:
             pl.semaphore_wait(barrier, n_gx - 1 + 4)
-            start(z_copies(r))
+        start(z_copies(r))
+        finish_src()
+        pack_y(r, src)
         start(y_copies(r))
         ours = src[:, pl.ds(near_row, 2)]
         for k in range(2):
@@ -751,19 +781,46 @@
         y_fix(r)
         for i in range(cx):
             acc[:, i] -= vel[n, 1, i] * yside[:, i]
+        closing = close()
+        settle(r - 1)
+        z_both(r).wait_recv()
+        return closing(uz_pack[n] * z_fix(r))
+
+    def close_state():
         before = packed(rows_of(acc))
-        z_both(r).wait_recv()
-        fix = uz_pack[n] * z_fix(r)
-        after = before - fix
-
-        def finish():
-            for i in range(cx):
-                dst[:, i] = acc[:, i] - unpacked(fix, i)
-
-        return after, finish
-
-    def adjoint(r, n, src, dst, edge, finish_src, extra):
-        settle(r - 2)
+
+        def closing(fix):
+            def finish():
+                for i in range(cx):
+                    state_one[:, i] = acc[:, i] - unpacked(fix, i)
+
+            return before - fix, finish
+
+        return closing
+
+    def close_observed():
+        groups = range(cx // WIN)
+        before = None
+        for g in groups:
+            sums = fold([acc[:, g * WIN + k] for k in range(WIN)]).reshape(comps * cy, cz)
+            both = apply(sums, seen_w[g])
+            mixed[g] = both[:, :cz]
+            before = both[:, cz:] if before is None else before + both[:, cz:]
+
+        def closing(fix):
+            flat = fix.reshape(comps * cy, cz)
+
+            def finish():
+                for g in groups:
+                    total = (mixed[g] - apply(flat, fix_rows[g])).reshape(comps, cy, cz)
+                    for k, t in enumerate(unfold(total)):
+                        force[:, g * WIN + k] = t
+
+            return (before - apply(flat, fix_edge[...])).reshape(comps, cy, cz), finish
+
+        return closing
+
+    def adjoint(r, n, src, dst, edge, finish_src, shadow, extra):
         zsend[r] = uz_pack[n] * edge
         start(z_copies(r))
         finish_src()
@@ -777,6 +834,7 @@
             xsend[r, k] = weighted([(local_s[j, near_row + k], rhs[:, j]) for j in range(cx)])
             xsend[r, 2 + k] = weighted([(out_s[k, j], rhs[:, j]) for j in range(cx)])
         x_copy(r).start()
+        shadow()
         for i in range(cx):
             held[:, i] = weighted([(local_s[j, i], rhs[:, j]) for j in range(cx)])
         for i in range(cx):
@@ -808,6 +866,7 @@
         for i in range(cx):
             acc[:, i] += yside[:, i]
         before = packed(rows_of(acc))
+        settle(r - 1)
         z_both(r).wait_recv()
         fix = z_fix(r)
         after = before + fix
@@ -825,20 +884,22 @@
         copy.wait()
 
     def observe_one():
+        observe(state_one, obs)
+
+    def tables():
         win_copy.wait_recv()
         build_blocks()
-        observe(state_one, obs)
+        build_edges()
+
+    def nothing():
+        pass
 
     loads[0].wait()
-    edge, finish = tangent(0, 0, dir_ref, state_one, packed(rows_of(dir_ref)), table)
+    edge, finish = tangent(0, 0, dir_ref, packed(rows_of(dir_ref)), nothing, table, close_state)
+    edge, finish = tangent(1, 1, state_one, edge, finish, tables, close_observed)
+    edge, finish = adjoint(2, 1, force, costate, edge, finish, observe_one, obs)
+    edge, finish = adjoint(3, 0, costate, res_ref, edge, finish, nothing, None)
     finish()
-    edge, finish = tangent(1, 1, state_one, state_two, edge, observe_one)
-    finish()
-    observe(state_two, force)
-    edge, finish = adjoint(2, 1, force, state_two, packed(rows_of(force)), lambda: None, obs)
-    edge, finish = adjoint(3, 0, state_two, res_ref, edge, finish, None)
-    finish()
-    settle(2)
     settle(3)
     win_copy.wait_send()
     table_copy.wait_send()
@@ -885,6 +946,9 @@
                     held(4, 2, wide, comps, cx, cz), held(4, 2, wide, comps, cx, cz),
                     held(4, comps, cy, cz), held(4, 2, comps, cy, cz),
                     held(owned, count, count), held(n_gx * owned, count, cz), held(cx // WIN, count * WIN, cz),
+                    pltpu.VMEM((cx // WIN, 3 * cz, 2 * cz), jnp.bfloat16),
+                    pltpu.VMEM((cx // WIN, 3 * cz, cz), jnp.bfloat16), pltpu.VMEM((3 * cz, cz), jnp.bfloat16),
+                    held(cx // WIN, comps * cy, cz),
                     sems((10,)), sems((4,)),
                 ] + [sems((2,))] * 6,
             )(*operands)

time: 22.6 us -> 22.3 us (0.987)
    pallas_call x1, Pallas kernels: 21.7 us -> 21.5 us  [local(): call(functools.partial(pair_kernel, sizes), scratch_shapes=loaded + [held...]
where the time goes in v2:
time: 22.3 us; the launch traced here: 22.2 us
  Pallas kernels  21.5 us (96%)
  other arithmetic  0.7 us (3%)
    pallas_call x1, Pallas kernels, local(): call(functools.partial(pair_kernel, sizes), scratch_shapes=loaded + [held...  21.5 us
    add x1, other arithmetic, local(): return pulled + direction  0.7 us

profile of v2, /device:TPU:0, one launch (start us, length us, event | category | flops | bytes accessed | tf_op | source)
XLA Modules:
  0.0 22.2 jit_solution(3187237248162845587)
XLA Ops:
  0.0 0.0 copy-start
  0.0 21.5 %shard_map.91 = f32[3,16,8,128]{3,2,1,0:T(8,128)S(1)} custom-call(f32[3,16,8,128]{3,2,1,0:T(8,128)} %dir_hbm.1, bf16[2,3,16,8,128]{4,3,2,1,0:T(8,128)(2,1)} %base_hbm.1, f32[4,16,16]{2,1,0:T(8,128)} %bitcast.2, f32[16,16]{1,0:T(8,128)} %local_h.1, f32[2,16]{1,0:T(2,128)} %in_h.1, f32[2,16]{1,0:T(2,128)} %bitcast.3, f32[4,4]{1,0:T(4,128)} %schur_h.1, ...), custom_call_target="tpu_custom_call" | custom-call | tf_op jit(solution)/shard_map/pallas_call | solution.py:939
  21.5 0.0 copy-done
  21.5 0.7 %add.3 = f32[3,16,8,128]{3,2,1,0:T(8,128)} add(f32[3,16,8,128]{3,2,1,0:T(8,128)S(1)} %shard_map.91, f32[3,16,8,128]{3,2,1,0:T(8,128)S(1)} %copy-done) | non-fusion elementwise | flops 49152 | bytes 589824 | tf_op jit(solution)/shard_map/add | solution.py:955
Async XLA Ops:
  0.0 21.5 %copy-start = (f32[3,16,8,128]{3,2,1,0:T(8,128)S(1)}, f32[3,16,8,128]{3,2,1,0:T(8,128)}, u32[]{:S(2)}) copy-start(f32[3,16,8,128]{3,2,1,0:T(8,128)} %dir_hbm.1) | copy-start | bytes 589828

commit v3 on v2

--- a/solution.py
+++ b/solution.py
@@ -475,13 +475,14 @@
     res_ref,
     dir_ref, base_ref, inv_ref, local_s, in_s, out_s, schur_s, plane_s, slot_s, in_v, near_v, near_s,
     state_one, costate, force, acc, rhs, obs, prod, held, yside, vel, uz_pack,
-    xsend, xrecv, ysend, yrecv, zsend, zrecv, winrecv, lanes_inv, blocks, seen_w, fix_rows, fix_edge, mixed,
-    load_sem, side_sem, xs_sem, xr_sem, ys_sem, yr_sem, zs_sem, zr_sem,
+    xsend, xrecv, ysend, yrecv, zsend, zrecv, winrecv, lanes_inv, blocks, seen_w, fix_rows, fix_edge, mixed, uz_near,
+    own_side, fix_sent, fix_near, across_x, across_w, uxy_pack,
+    load_sem, sent_sem, side_sem, xr_sem, yr_sem, zr_sem,
 ):
     n_gx, n_gy, n_gz = sizes
     gx, gy, gz = lax.axis_index("gx"), lax.axis_index("gy"), lax.axis_index("gz")
     comps, cx, cy, cz = dir_ref.shape
-    wide = ysend.shape[2]
+    wide = ysend.shape[3]
     owned = inv_ref.shape[0]
     other = 1 - gx
     y_next, y_prev = lax.rem(gy + 1, n_gy), lax.rem(gy + n_gy - 1, n_gy)
@@ -513,39 +514,59 @@
             device_id=where, device_id_type=MESH,
         )
 
+    x_sent = [load_sem.at[n] for n in (1, 7, 1, 7)]
+    y_sent = [sent_sem.at[0], load_sem.at[6]] * 2
+    z_sent = [load_sem.at[n] for n in (0, 5, 0, 8)]
+
     def x_copy(r):
-        return remote(xsend.at[r], xrecv.at[r], xs_sem.at[r % 2], xr_sem.at[r % 2], {"gx": other})
-
-    def y_copies(r):
+        return remote(xsend.at[r], xrecv.at[r], x_sent[r], xr_sem.at[r % 2], {"gx": other})
+
+    def y_copies(r, c):
         return tuple(
-            remote(ysend.at[r, d], yrecv.at[r, d], ys_sem.at[r % 2], yr_sem.at[r % 2], {"gy": q})
+            remote(ysend.at[r, c, d], yrecv.at[r, c, d], y_sent[r], yr_sem.at[r % 2, c], {"gy": q})
             for d, q in enumerate((y_prev, y_next))
         )
 
     def z_copies(r):
         return tuple(
-            remote(zsend.at[r], zrecv.at[r, d], zs_sem.at[r % 2], zr_sem.at[r % 2], {"gz": q})
+            remote(zsend.at[r], zrecv.at[r, d], z_sent[r], zr_sem.at[r], {"gz": q})
             for d, q in enumerate((z_prev, z_next))
         )
 
-    def y_both(r):
-        return remote(yrecv.at[r], yrecv.at[r], ys_sem.at[r % 2], yr_sem.at[r % 2], {"gy": y_next})
+    uz_copies = tuple(
+        remote(uz_pack.at[0], uz_near.at[d], load_sem.at[4], side_sem.at[2], {"gz": q})
+        for d, q in enumerate((z_prev, z_next))
+    )
+    uz_both = remote(uz_near, uz_near, load_sem.at[4], side_sem.at[2], {"gz": z_next})
+
+    fix_copies = tuple(
+        remote(fix_sent, fix_near.at[d], load_sem.at[9], side_sem.at[3], where)
+        for d, where in enumerate(({"gy": y_prev}, {"gy": y_next}, {"gx": other}))
+    )
+    fix_all = remote(fix_near, fix_near, load_sem.at[9], side_sem.at[3], {"gx": other})
+
+    def y_both(r, c):
+        return remote(yrecv.at[r, c], yrecv.at[r, c], y_sent[r], yr_sem.at[r % 2, c], {"gy": y_next})
+
+    def y_all(r):
+        return remote(yrecv.at[r], yrecv.at[r], y_sent[r], yr_sem.at[r % 2, 0], {"gy": y_next})
 
     def z_both(r):
-        return remote(zrecv.at[r], zrecv.at[r], zs_sem.at[r % 2], zr_sem.at[r % 2], {"gz": z_next})
+        return remote(zrecv.at[r], zrecv.at[r], z_sent[r], zr_sem.at[r], {"gz": z_next})
 
     def settle(r):
         if r >= 0:
             x_copy(r).wait_send()
-            y_both(r).wait_send()
+            y_all(r).wait_send()
             z_both(r).wait_send()
 
-    win_copy = remote(inv_ref, winrecv, side_sem.at[0], side_sem.at[1], {"gx": other})
-    table_copy = remote(in_v, near_v, side_sem.at[2], side_sem.at[3], {"gx": other})
+    win_copy = remote(inv_ref, winrecv, load_sem.at[3], side_sem.at[0], {"gx": other})
+    table_copy = remote(in_v, near_v, load_sem.at[2], side_sem.at[1], {"gx": other})
 
     lane = lax.broadcasted_iota(jnp.int32, (cy, cz), 1)
     in_group = lane % WIN
     cell_of = ((lane + WIN // 2) // WIN) % cx
+    sub = lax.broadcasted_iota(jnp.int32, (cy, cz), 0)
     near_edge = (lane < 3) | (lane >= cz - 3)
     left, right = in_group < 3, in_group >= WIN - 3
     ahead = in_group < WIN // 2
@@ -562,12 +583,13 @@
         turned = block if i == 0 else pltpu.roll(block, (cz - WIN * i) % cz, 2)
         return jnp.where(near_edge, turned, 0.0)
 
-    def pack_y(r, src):
+    def send_y(r, src):
         lines = src.reshape(comps * cx * cy, cz)
-        for side, start in ((0, 0), (1, cy - wide)):
-            for m in range(wide):
-                for c in range(comps):
-                    ysend[r, side, m, c] = lines[pl.ds(c * cx * cy + start + m, cx, stride=cy), :]
+        for c in range(comps):
+            for side, begin in ((0, 0), (1, cy - wide)):
+                for m in range(wide):
+                    ysend[r, c, side, m] = lines[pl.ds(c * cx * cy + begin + m, cx, stride=cy), :]
+            start(y_copies(r, c))
 
     def circular(block, axis):
         size = block.shape[axis]
@@ -577,29 +599,32 @@
 
         return C1 * diff(1) + C2 * diff(2) + C3 * diff(3)
 
-    def z_fix(r):
-        delta = jnp.where(ahead, zrecv[r, 0], zrecv[r, 1]) - zsend[r]
-        low = jnp.where(right, delta, 0.0)
-        top = jnp.where(left, delta, 0.0)
+    def lateral(edge):
+        low = jnp.where(right, edge, 0.0)
+        top = jnp.where(left, edge, 0.0)
         low_fix = -(C1 * pltpu.roll(low, 1, 2) + C2 * pltpu.roll(low, 2, 2) + C3 * pltpu.roll(low, 3, 2))
         top_fix = (C1 * pltpu.roll(top, cz - 1, 2) + C2 * pltpu.roll(top, cz - 2, 2)
                    + C3 * pltpu.roll(top, cz - 3, 2))
         return jnp.where(left, low_fix, jnp.where(right, top_fix, 0.0))
 
-    def y_fix(r):
+    def facing(pair):
+        return jnp.where(ahead, pair[0], pair[1])
+
+    def y_fix(r, c):
+        y_both(r, c).wait_recv()
         lines = yside.reshape(comps * cx * cy, cz)
-        for c in range(comps):
-            def put(row, value):
-                lines[pl.ds(c * cx * cy + row, cx, stride=cy), :] = value
-
-            d0, d1, d2 = (yrecv[r, 0, m, c] - ysend[r, 0, m, c] for m in range(3))
-            put(cy - 1, C1 * d0 + C2 * d1 + C3 * d2)
-            put(cy - 2, C2 * d0 + C3 * d1)
-            put(cy - 3, C3 * d0)
-            d0, d1, d2 = (yrecv[r, 1, m, c] - ysend[r, 1, m, c] for m in range(3))
-            put(0, -(C1 * d2 + C2 * d1 + C3 * d0))
-            put(1, -(C2 * d2 + C3 * d1))
-            put(2, -(C3 * d2))
+
+        def put(row, value):
+            lines[pl.ds(c * cx * cy + row, cx, stride=cy), :] = value
+
+        d0, d1, d2 = (yrecv[r, c, 0, m] - ysend[r, c, 0, m] for m in range(3))
+        put(cy - 1, C1 * d0 + C2 * d1 + C3 * d2)
+        put(cy - 2, C2 * d0 + C3 * d1)
+        put(cy - 3, C3 * d0)
+        d0, d1, d2 = (yrecv[r, c, 1, m] - ysend[r, c, 1, m] for m in range(3))
+        put(0, -(C1 * d2 + C2 * d1 + C3 * d0))
+        put(1, -(C2 * d2 + C3 * d1))
+        put(2, -(C3 * d2))
 
     def stencil_inside(row, i):
         total = None
@@ -721,27 +746,60 @@
         for copy in copies:
             copy.start()
 
-    def tangent(r, n, src, edge, finish_src, shadow, close):
-        zsend[r] = edge
-        if not r:
-            pl.semaphore_wait(barrier, n_gx - 1 + 4)
-        start(z_copies(r))
-        finish_src()
-        pack_y(r, src)
-        start(y_copies(r))
+    def send_sides(r, src):
         ours = src[:, pl.ds(near_row, 2)]
         for k in range(2):
             xsend[r, k] = ours[:, k]
-        if not r:
-            loads[2].wait()
-            table_copy.start()
-            loads[1].wait()
         for i in range(cx):
             rhs[:, i] = stencil_inside(rows_of(src), i)
         for k in range(2):
             xsend[r, 2 + k] = weighted([(in_s[k, j], rhs[:, j]) for j in range(cx)])
         x_copy(r).start()
+
+    def build_across():
+        def spot(j):
+            return jnp.where(cell_of == j, 1.0, 0.0)
+
+        corner = across((spot(their_row), spot(their_row + 1)), first)
+        inner = [stencil_inside(spot, j) for j in range(cx)]
+        own = [in_s[k, near_row] * corner[0] + in_s[k, near_row + 1] * corner[1] for k in range(2)]
+        theirs = [weighted([(near_s[k, j], inner[j]) for j in range(cx)]) for k in range(2)]
+        values = [
+            weighted([(schur_s[2 * gx + m, 2 * gx + k], own[k]) for k in range(2)]
+                     + [(schur_s[2 * gx + m, 2 * other + k], theirs[k]) for k in range(2)])
+            for m in range(2)
+        ]
+        lines = [
+            weighted([(local_s[i, near_row], corner[0]), (local_s[i, near_row + 1], corner[1]),
+                      (out_s[0, i], values[0]), (out_s[1, i], values[1])])
+            for i in range(cx)
+        ]
+        for i in range(cx):
+            line = jnp.where(sub < WIN // 2, lines[i], lines[(i + 1) % cx])
+            across_x[i * WIN : (i + 1) * WIN] = jnp.where(in_group == sub, line, 0.0)
+        across_w[...] = weights(across_x[...].T)
+
+    def side_fix():
+        fix_all.wait_recv()
+        along_x = apply(fix_near[2].reshape(comps * cy, cz), across_w[...]).reshape(comps, cy, cz)
+        after_y, before_y = fix_near[0] - fix_sent[...], fix_near[1] - fix_sent[...]
+        along_y = weighted([
+            (coef, pltpu.roll(jnp.where(sub < k, after_y, 0.0), cy - k, 1)
+             - pltpu.roll(jnp.where(sub >= cy - k, before_y, 0.0), k, 1))
+            for k, coef in ((1, C1), (2, C2), (3, C3))
+        ])
+        return uxy_pack[0] * along_x + uxy_pack[1] * along_y
+
+    def tangent(r, n, src, edge, before_face, finish_src, shadow, close):
         if not r:
+            zsend[r] = edge
+            pl.semaphore_wait(barrier, n_gx - 1 + 4)
+            start(z_copies(r))
+            send_y(r, src)
+            loads[2].wait()
+            table_copy.start()
+            loads[1].wait()
+            send_sides(r, src)
             for copy in loads[3:]:
                 copy.wait()
             win_copy.start()
@@ -750,20 +808,40 @@
                     for i in range(cx):
                         vel[m, c, i] = time_step * base_ref[m, c, i].astype(jnp.float32)
                 uz_pack[m] = packed(lambda i: vel[m, 2, i])
+                if not m:
+                    start(uz_copies)
             yside[...] = jnp.zeros(yside.shape, jnp.float32)
+            ends = xsend[r, 0], xsend[r, 1]
+            sides = [xsend.at[r, 2 + k] for k in range(2)]
+        else:
+            finish_src()
+            for i in range(cx):
+                rhs[:, i] = stencil_inside(rows_of(src), i)
+            for k in range(2):
+                own_side[k] = weighted([(in_s[k, j], rhs[:, j]) for j in range(cx)])
+            ours = src[:, pl.ds(near_row, 2)]
+            ends = ours[:, 0], ours[:, 1]
+            sides = [own_side.at[k] for k in range(2)]
         for i in range(cx):
             block = src[:, i]
             solved = weighted([(local_s[i, j], rhs[:, j]) for j in range(cx)])
             acc[:, i] = block - (
                 vel[n, 2, i] * circular(block, 2) + vel[n, 1, i] * circular(block, 1) + vel[n, 0, i] * solved)
         shadow()
+        away = across(ends, gx != 0)
+        face = lateral(edge)
+        def add_y(c):
+            y_fix(r, c)
+            for i in range(cx):
+                acc[c, i] -= vel[n, 1, i] * yside[c, i]
+
+        for c in range(comps - 1):
+            add_y(c)
         x_copy(r).wait_recv()
-        pair = xrecv[r, 0], xrecv[r, 1]
-        halo = across(pair, first)
+        halo = across((xrecv[r, 0], xrecv[r, 1]), first)
         own = [
-            xsend[r, 2 + k] + in_s[k, near_row] * halo[0] + in_s[k, near_row + 1] * halo[1] for k in range(2)
+            sides[k][...] + in_s[k, near_row] * halo[0] + in_s[k, near_row + 1] * halo[1] for k in range(2)
         ]
-        away = across((xsend[r, 0], xsend[r, 1]), gx != 0)
         theirs = [
             xrecv[r, 2 + k] + near_s[k, their_row] * away[0] + near_s[k, their_row + 1] * away[1]
             for k in range(2)
@@ -777,28 +855,36 @@
             acc[:, i] -= vel[n, 0, i] * weighted([
                 (local_s[i, near_row], halo[0]), (local_s[i, near_row + 1], halo[1]),
                 (out_s[0, i], values[0]), (out_s[1, i], values[1])])
-        y_both(r).wait_recv()
-        y_fix(r)
-        for i in range(cx):
-            acc[:, i] -= vel[n, 1, i] * yside[:, i]
-        closing = close()
-        settle(r - 1)
+        add_y(comps - 1)
+        closing = close(face)
+        if r:
+            uz_both.wait_recv()
+            missing = facing(uz_near) * before_face
         z_both(r).wait_recv()
-        return closing(uz_pack[n] * z_fix(r))
-
-    def close_state():
-        before = packed(rows_of(acc))
-
-        def closing(fix):
+        theirs = facing(zrecv.at[r])
+        return closing(lateral(theirs - missing if r else theirs)), face
+
+    def close_state(face):
+        before = packed(rows_of(acc)) + uz_pack[0] * face
+        zsend[1] = before
+        start(z_copies(1))
+        send_y(1, acc)
+        send_sides(1, acc)
+
+        def closing(late):
+            fix = uz_pack[0] * (late - face)
+            fix_sent[...] = fix
+            start(fix_copies)
+
             def finish():
                 for i in range(cx):
                     state_one[:, i] = acc[:, i] - unpacked(fix, i)
 
-            return before - fix, finish
+            return before - uz_pack[0] * late, finish
 
         return closing
 
-    def close_observed():
+    def close_observed(face):
         groups = range(cx // WIN)
         before = None
         for g in groups:
@@ -807,8 +893,10 @@
             mixed[g] = both[:, :cz]
             before = both[:, cz:] if before is None else before + both[:, cz:]
 
-        def closing(fix):
-            flat = fix.reshape(comps * cy, cz)
+        settle(0)
+
+        def closing(late):
+            flat = (uz_pack[1] * (late - face) - side_fix()).reshape(comps * cy, cz)
 
             def finish():
                 for g in groups:
@@ -820,14 +908,15 @@
 
         return closing
 
-    def adjoint(r, n, src, dst, edge, finish_src, shadow, extra):
-        zsend[r] = uz_pack[n] * edge
-        start(z_copies(r))
+    def adjoint(r, n, src, dst, edge, before_face, finish_src, shadow, extra):
+        edge = uz_pack[n] * edge
+        if before_face is None:
+            zsend[r] = edge
+            start(z_copies(r))
         finish_src()
         for i in range(cx):
             prod[:, i] = vel[n, 1, i] * src[:, i]
-        pack_y(r, prod)
-        start(y_copies(r))
+        send_y(r, prod)
         for i in range(cx):
             rhs[:, i] = vel[n, 0, i] * src[:, i]
         for k in range(2):
@@ -842,6 +931,14 @@
             if extra is not None:
                 total = total + extra[:, i]
             acc[:, i] = total + stencil_inside(rows_of(held), i)
+
+        def add_y(c):
+            y_fix(r, c)
+            for i in range(cx):
+                acc[c, i] += yside[c, i]
+
+        for c in range(comps - 1):
+            add_y(c)
         x_copy(r).wait_recv()
 
         def solved(block):
@@ -861,25 +958,30 @@
                 (stencil_inside(lambda j, m=m: in_s[m, j], i), own[m]) for m in range(2)])
         for k in range(2):
             acc[:, near_row + k] += halo[k]
-        y_both(r).wait_recv()
-        y_fix(r)
-        for i in range(cx):
-            acc[:, i] += yside[:, i]
-        before = packed(rows_of(acc))
+        add_y(comps - 1)
+        face = lateral(edge)
+        if before_face is None:
+            before = packed(rows_of(acc)) - face
+            zsend[r + 1] = uz_pack[n - 1] * before
+            start(z_copies(r + 1))
+        else:
+            missing = facing(uz_near) * before_face
         settle(r - 1)
         z_both(r).wait_recv()
-        fix = z_fix(r)
-        after = before + fix
+        theirs = facing(zrecv.at[r])
+        late = lateral(theirs if before_face is None else theirs + missing)
+        fix = late - face
+        after = before + late if before_face is None else None
 
         def finish():
             for i in range(cx):
                 dst[:, i] = acc[:, i] + unpacked(fix, i)
 
-        return after, finish
+        return after, face, finish
 
     def table():
         table_copy.wait_recv()
-        copy = pltpu.make_async_copy(near_v, near_s, load_sem.at[0])
+        copy = pltpu.make_async_copy(near_v, near_s, load_sem.at[8])
         copy.start()
         copy.wait()
 
@@ -890,18 +992,24 @@
         win_copy.wait_recv()
         build_blocks()
         build_edges()
+        build_across()
+        for c in range(2):
+            uxy_pack[c] = packed(lambda i: vel[1, c, i])
 
     def nothing():
         pass
 
     loads[0].wait()
-    edge, finish = tangent(0, 0, dir_ref, packed(rows_of(dir_ref)), nothing, table, close_state)
-    edge, finish = tangent(1, 1, state_one, edge, finish, tables, close_observed)
-    edge, finish = adjoint(2, 1, force, costate, edge, finish, observe_one, obs)
-    edge, finish = adjoint(3, 0, costate, res_ref, edge, finish, nothing, None)
+    (edge, finish), face = tangent(
+        0, 0, dir_ref, packed(rows_of(dir_ref)), None, nothing, table, close_state)
+    (edge, finish), face = tangent(1, 1, state_one, edge, face, finish, tables, close_observed)
+    edge, face, finish = adjoint(2, 1, force, costate, edge, None, finish, observe_one, obs)
+    edge, face, finish = adjoint(3, 0, costate, res_ref, edge, face, finish, nothing, dir_ref)
     finish()
     settle(3)
     win_copy.wait_send()
+    uz_both.wait_send()
+    fix_all.wait_send()
     table_copy.wait_send()
 
 
@@ -943,16 +1051,18 @@
                 ] + [field] * 9 + [
                     held(*base_flow.shape), held(2, cy, cz),
                     held(4, 4, comps, cy, cz), held(4, 4, comps, cy, cz),
-                    held(4, 2, wide, comps, cx, cz), held(4, 2, wide, comps, cx, cz),
+                    held(4, comps, 2, wide, cx, cz), held(4, comps, 2, wide, cx, cz),
                     held(4, comps, cy, cz), held(4, 2, comps, cy, cz),
                     held(owned, count, count), held(n_gx * owned, count, cz), held(cx // WIN, count * WIN, cz),
                     pltpu.VMEM((cx // WIN, 3 * cz, 2 * cz), jnp.bfloat16),
                     pltpu.VMEM((cx // WIN, 3 * cz, cz), jnp.bfloat16), pltpu.VMEM((3 * cz, cz), jnp.bfloat16),
-                    held(cx // WIN, comps * cy, cz),
-                    sems((10,)), sems((4,)),
-                ] + [sems((2,))] * 6,
+                    held(cx // WIN, comps * cy, cz), held(2, cy, cz),
+                    held(2, comps, cy, cz), held(comps, cy, cz), held(3, comps, cy, cz),
+                    held(cz, cz), pltpu.VMEM((3 * cz, cz), jnp.bfloat16), held(2, cy, cz),
+                    sems((10,)), sems((1,)), sems((4,)), sems((2,)), sems((2, comps)), sems((4,)),
+                ],
             )(*operands)
-            return pulled + direction
+            return pulled
         pulled = call(
             functools.partial(kernel, sizes),
             scratch_shapes=loaded + [

time: 22.3 us -> 22.2 us (level)
  other arithmetic: 0.7 us -> 0 us
  local copies, waits for them, and re-layouts: 0.01 us -> 0.68 us
    add x1 -> x0, other arithmetic: 0.7 us -> none  [local(): return pulled + direction]
    unnamed x2 -> x1, local copies, waits for them, and re-layouts: 0.01 us -> 0.68 us
where the time goes in v3:
time: 22.2 us; the launch traced here: 22 us
  Pallas kernels  21.3 us (96%)
  local copies, waits for them, and re-layouts  0.68 us (3%)
    pallas_call x1, Pallas kernels, local(): call(functools.partial(pair_kernel, sizes), scratch_shapes=loaded + [held...  21.3 us
    unnamed x1, local copies, waits for them, and re-layouts  0.68 us

profile of v3, /device:TPU:0, one launch (start us, length us, event | category | flops | bytes accessed | tf_op | source)
XLA Modules:
  0.0 22.0 jit_solution(7823683708181718229)
XLA Ops:
  0.0 21.3 %shard_map.91 = f32[3,16,8,128]{3,2,1,0:T(8,128)S(1)} custom-call(f32[3,16,8,128]{3,2,1,0:T(8,128)} %dir_hbm.1, bf16[2,3,16,8,128]{4,3,2,1,0:T(8,128)(2,1)} %base_hbm.1, f32[4,16,16]{2,1,0:T(8,128)} %bitcast.2, f32[16,16]{1,0:T(8,128)} %local_h.1, f32[2,16]{1,0:T(2,128)} %in_h.1, f32[2,16]{1,0:T(2,128)} %bitcast.3, f32[4,4]{1,0:T(4,128)} %schur_h.1, ...), custom_call_target="tpu_custom_call" | custom-call | tf_op jit(solution)/shard_map/pallas_call | solution.py:1047
  21.4 0.7 %copy.11 = f32[3,16,8,128]{3,2,1,0:T(8,128)} copy(f32[3,16,8,128]{3,2,1,0:T(8,128)S(1)} %shard_map.91) | data formatting | bytes 393216

commit v4 on v3

--- a/solution.py
+++ b/solution.py
@@ -473,7 +473,7 @@
     dir_hbm, base_hbm, inv_hbm,
     local_h, in_h, out_h, schur_h, plane_h, slot_h,
     res_ref,
-    dir_ref, base_ref, inv_ref, local_s, in_s, out_s, schur_s, plane_s, slot_s, in_v, near_v, near_s,
+    dir_ref, base_ref, inv_ref, local_s, in_s, out_s, schur_s, plane_s, slot_s, in_v, near_v, near_s, slope_s,
     state_one, costate, force, acc, rhs, obs, prod, held, yside, vel, uz_pack,
     xsend, xrecv, ysend, yrecv, zsend, zrecv, winrecv, lanes_inv, blocks, seen_w, fix_rows, fix_edge, mixed, uz_near,
     own_side, fix_sent, fix_near, across_x, across_w, uxy_pack,
@@ -518,8 +518,11 @@
     y_sent = [sent_sem.at[0], load_sem.at[6]] * 2
     z_sent = [load_sem.at[n] for n in (0, 5, 0, 8)]
 
-    def x_copy(r):
-        return remote(xsend.at[r], xrecv.at[r], x_sent[r], xr_sem.at[r % 2], {"gx": other})
+    def x_copy(r, c):
+        return remote(xsend.at[r, c], xrecv.at[r, c], x_sent[r], xr_sem.at[r % 2, c], {"gx": other})
+
+    def x_all(r):
+        return remote(xsend.at[r], xrecv.at[r], x_sent[r], xr_sem.at[r % 2, 0], {"gx": other})
 
     def y_copies(r, c):
         return tuple(
@@ -556,7 +559,7 @@
 
     def settle(r):
         if r >= 0:
-            x_copy(r).wait_send()
+            x_all(r).wait_send()
             y_all(r).wait_send()
             z_both(r).wait_send()
 
@@ -583,13 +586,12 @@
         turned = block if i == 0 else pltpu.roll(block, (cz - WIN * i) % cz, 2)
         return jnp.where(near_edge, turned, 0.0)
 
-    def send_y(r, src):
+    def send_y(r, c, src):
         lines = src.reshape(comps * cx * cy, cz)
-        for c in range(comps):
-            for side, begin in ((0, 0), (1, cy - wide)):
-                for m in range(wide):
-                    ysend[r, c, side, m] = lines[pl.ds(c * cx * cy + begin + m, cx, stride=cy), :]
-            start(y_copies(r, c))
+        for side, begin in ((0, 0), (1, cy - wide)):
+            for m in range(wide):
+                ysend[r, c, side, m] = lines[pl.ds(c * cx * cy + begin + m, cx, stride=cy), :]
+        start(y_copies(r, c))
 
     def circular(block, axis):
         size = block.shape[axis]
@@ -641,8 +643,8 @@
             total = part if total is None else total + part
         return total
 
-    def rows_of(ref):
-        return lambda i: ref[:, i]
+    def rows_of(ref, c=slice(None)):
+        return lambda i: ref[c, i]
 
     def across(pair, to_first):
         low, high = pair
@@ -746,15 +748,13 @@
         for copy in copies:
             copy.start()
 
-    def send_sides(r, src):
-        ours = src[:, pl.ds(near_row, 2)]
+    def send_sides(r, c, src):
+        xsend[r, c, 0:2] = src[c, pl.ds(near_row, 2)]
+        for i in range(cx):
+            rhs[c, i] = stencil_inside(rows_of(src, c), i)
         for k in range(2):
-            xsend[r, k] = ours[:, k]
-        for i in range(cx):
-            rhs[:, i] = stencil_inside(rows_of(src), i)
-        for k in range(2):
-            xsend[r, 2 + k] = weighted([(in_s[k, j], rhs[:, j]) for j in range(cx)])
-        x_copy(r).start()
+            xsend[r, c, 2 + k] = weighted([(in_s[k, j], rhs[c, j]) for j in range(cx)])
+        x_copy(r, c).start()
 
     def build_across():
         def spot(j):
@@ -795,11 +795,13 @@
             zsend[r] = edge
             pl.semaphore_wait(barrier, n_gx - 1 + 4)
             start(z_copies(r))
-            send_y(r, src)
+            for c in range(comps):
+                send_y(r, c, src)
             loads[2].wait()
             table_copy.start()
             loads[1].wait()
-            send_sides(r, src)
+            for c in range(comps):
+                send_sides(r, c, src)
             for copy in loads[3:]:
                 copy.wait()
             win_copy.start()
@@ -811,51 +813,50 @@
                 if not m:
                     start(uz_copies)
             yside[...] = jnp.zeros(yside.shape, jnp.float32)
-            ends = xsend[r, 0], xsend[r, 1]
-            sides = [xsend.at[r, 2 + k] for k in range(2)]
+            for m in range(2):
+                for i in range(cx):
+                    slope_s[m, i] = stencil_inside(lambda j: in_s[m, j], i)
         else:
             finish_src()
             for i in range(cx):
                 rhs[:, i] = stencil_inside(rows_of(src), i)
             for k in range(2):
                 own_side[k] = weighted([(in_s[k, j], rhs[:, j]) for j in range(cx)])
-            ours = src[:, pl.ds(near_row, 2)]
-            ends = ours[:, 0], ours[:, 1]
-            sides = [own_side.at[k] for k in range(2)]
         for i in range(cx):
             block = src[:, i]
             solved = weighted([(local_s[i, j], rhs[:, j]) for j in range(cx)])
             acc[:, i] = block - (
                 vel[n, 2, i] * circular(block, 2) + vel[n, 1, i] * circular(block, 1) + vel[n, 0, i] * solved)
         shadow()
-        away = across(ends, gx != 0)
         face = lateral(edge)
-        def add_y(c):
+        for c in range(comps):
+            away = across([src[c, near_row + k] for k in range(2)], gx != 0)
+            sides = [own_side[k, c] if r else xsend[r, c, 2 + k] for k in range(2)]
+            x_copy(r, c).wait_recv()
+            halo = across((xrecv[r, c, 0], xrecv[r, c, 1]), first)
+            own = [
+                sides[k] + in_s[k, near_row] * halo[0] + in_s[k, near_row + 1] * halo[1] for k in range(2)
+            ]
+            theirs = [
+                xrecv[r, c, 2 + k] + near_s[k, their_row] * away[0] + near_s[k, their_row + 1] * away[1]
+                for k in range(2)
+            ]
+            values = [
+                weighted([(schur_s[2 * gx + m, 2 * gx + k], own[k]) for k in range(2)]
+                         + [(schur_s[2 * gx + m, 2 * other + k], theirs[k]) for k in range(2)])
+                for m in range(2)
+            ]
             y_fix(r, c)
             for i in range(cx):
-                acc[c, i] -= vel[n, 1, i] * yside[c, i]
-
-        for c in range(comps - 1):
-            add_y(c)
-        x_copy(r).wait_recv()
-        halo = across((xrecv[r, 0], xrecv[r, 1]), first)
-        own = [
-            sides[k][...] + in_s[k, near_row] * halo[0] + in_s[k, near_row + 1] * halo[1] for k in range(2)
-        ]
-        theirs = [
-            xrecv[r, 2 + k] + near_s[k, their_row] * away[0] + near_s[k, their_row + 1] * away[1]
-            for k in range(2)
-        ]
-        values = [
-            weighted([(schur_s[2 * gx + m, 2 * gx + k], own[k]) for k in range(2)]
-                     + [(schur_s[2 * gx + m, 2 * other + k], theirs[k]) for k in range(2)])
-            for m in range(2)
-        ]
-        for i in range(cx):
-            acc[:, i] -= vel[n, 0, i] * weighted([
-                (local_s[i, near_row], halo[0]), (local_s[i, near_row + 1], halo[1]),
-                (out_s[0, i], values[0]), (out_s[1, i], values[1])])
-        add_y(comps - 1)
+                acc[c, i] -= vel[n, 1, i] * yside[c, i] + vel[n, 0, i] * weighted([
+                    (local_s[i, near_row], halo[0]), (local_s[i, near_row + 1], halo[1]),
+                    (out_s[0, i], values[0]), (out_s[1, i], values[1])])
+            if not r:
+                zsend[1, c] = packed(rows_of(acc, c)) + uz_pack[0] * face[c]
+                if c == comps - 1:
+                    start(z_copies(1))
+                send_y(1, c, acc)
+                send_sides(1, c, acc)
         closing = close(face)
         if r:
             uz_both.wait_recv()
@@ -865,11 +866,7 @@
         return closing(lateral(theirs - missing if r else theirs)), face
 
     def close_state(face):
-        before = packed(rows_of(acc)) + uz_pack[0] * face
-        zsend[1] = before
-        start(z_copies(1))
-        send_y(1, acc)
-        send_sides(1, acc)
+        before = zsend[1]
 
         def closing(late):
             fix = uz_pack[0] * (late - face)
@@ -898,13 +895,16 @@
         def closing(late):
             flat = (uz_pack[1] * (late - face) - side_fix()).reshape(comps * cy, cz)
 
+            edge = (before - apply(flat, fix_edge[...])).reshape(comps, cy, cz)
+            for g in groups:
+                mixed[g] = mixed[g] - apply(flat, fix_rows[g])
+
             def finish():
                 for g in groups:
-                    total = (mixed[g] - apply(flat, fix_rows[g])).reshape(comps, cy, cz)
-                    for k, t in enumerate(unfold(total)):
+                    for k, t in enumerate(unfold(mixed[g].reshape(comps, cy, cz))):
                         force[:, g * WIN + k] = t
 
-            return (before - apply(flat, fix_edge[...])).reshape(comps, cy, cz), finish
+            return edge, finish
 
         return closing
 
@@ -914,16 +914,18 @@
             zsend[r] = edge
             start(z_copies(r))
         finish_src()
-        for i in range(cx):
-            prod[:, i] = vel[n, 1, i] * src[:, i]
-        send_y(r, prod)
-        for i in range(cx):
-            rhs[:, i] = vel[n, 0, i] * src[:, i]
-        for k in range(2):
-            xsend[r, k] = weighted([(local_s[j, near_row + k], rhs[:, j]) for j in range(cx)])
-            xsend[r, 2 + k] = weighted([(out_s[k, j], rhs[:, j]) for j in range(cx)])
-        x_copy(r).start()
+        for c in range(comps):
+            for i in range(cx):
+                prod[c, i] = vel[n, 1, i] * src[c, i]
+            send_y(r, c, prod)
+            for i in range(cx):
+                rhs[c, i] = vel[n, 0, i] * src[c, i]
+            for k in range(2):
+                xsend[r, c, k] = weighted([(local_s[j, near_row + k], rhs[c, j]) for j in range(cx)])
+                xsend[r, c, 2 + k] = weighted([(out_s[k, j], rhs[c, j]) for j in range(cx)])
+            x_copy(r, c).start()
         shadow()
+        face = lateral(edge)
         for i in range(cx):
             held[:, i] = weighted([(local_s[j, i], rhs[:, j]) for j in range(cx)])
         for i in range(cx):
@@ -931,38 +933,30 @@
             if extra is not None:
                 total = total + extra[:, i]
             acc[:, i] = total + stencil_inside(rows_of(held), i)
-
-        def add_y(c):
+        for c in range(comps):
+            x_copy(r, c).wait_recv()
+
+            def solved(block):
+                return [
+                    weighted([(schur_s[2 * gx + k, 2 * block + m], xsend[r, c, 2 + k]) for k in range(2)]
+                             + [(schur_s[2 * other + k, 2 * block + m], xrecv[r, c, 2 + k]) for k in range(2)])
+                    for m in range(2)
+                ]
+
+            own, theirs = solved(gx), solved(other)
+            halo = across([
+                xrecv[r, c, k] + near_s[0, their_row + k] * theirs[0] + near_s[1, their_row + k] * theirs[1]
+                for k in range(2)
+            ], first)
+            for k in range(2):
+                acc[c, near_row + k] += halo[k]
             y_fix(r, c)
             for i in range(cx):
-                acc[c, i] += yside[c, i]
-
-        for c in range(comps - 1):
-            add_y(c)
-        x_copy(r).wait_recv()
-
-        def solved(block):
-            return [
-                weighted([(schur_s[2 * gx + k, 2 * block + m], xsend[r, 2 + k]) for k in range(2)]
-                         + [(schur_s[2 * other + k, 2 * block + m], xrecv[r, 2 + k]) for k in range(2)])
-                for m in range(2)
-            ]
-
-        own, theirs = solved(gx), solved(other)
-        halo = across([
-            xrecv[r, k] + near_s[0, their_row + k] * theirs[0] + near_s[1, their_row + k] * theirs[1]
-            for k in range(2)
-        ], first)
-        for i in range(cx):
-            acc[:, i] += weighted([
-                (stencil_inside(lambda j, m=m: in_s[m, j], i), own[m]) for m in range(2)])
-        for k in range(2):
-            acc[:, near_row + k] += halo[k]
-        add_y(comps - 1)
-        face = lateral(edge)
+                acc[c, i] += yside[c, i] + weighted([(slope_s[m, i], own[m]) for m in range(2)])
+            if before_face is None:
+                own_side[0, c] = packed(rows_of(acc, c)) - face[c]
+                zsend[r + 1, c] = uz_pack[n - 1] * own_side[0, c]
         if before_face is None:
-            before = packed(rows_of(acc)) - face
-            zsend[r + 1] = uz_pack[n - 1] * before
             start(z_copies(r + 1))
         else:
             missing = facing(uz_near) * before_face
@@ -971,7 +965,7 @@
         theirs = facing(zrecv.at[r])
         late = lateral(theirs if before_face is None else theirs + missing)
         fix = late - face
-        after = before + late if before_face is None else None
+        after = own_side[0] + late if before_face is None else None
 
         def finish():
             for i in range(cx):
@@ -1047,10 +1041,10 @@
             pulled = call(
                 functools.partial(pair_kernel, sizes),
                 scratch_shapes=loaded + [
-                    held(2, cx), held(2, cx), pltpu.SMEM((2, cx), jnp.float32),
+                    held(2, cx), held(2, cx), pltpu.SMEM((2, cx), jnp.float32), pltpu.SMEM((2, cx), jnp.float32),
                 ] + [field] * 9 + [
                     held(*base_flow.shape), held(2, cy, cz),
-                    held(4, 4, comps, cy, cz), held(4, 4, comps, cy, cz),
+                    held(4, comps, 4, cy, cz), held(4, comps, 4, cy, cz),
                     held(4, comps, 2, wide, cx, cz), held(4, comps, 2, wide, cx, cz),
                     held(4, comps, cy, cz), held(4, 2, comps, cy, cz),
                     held(owned, count, count), held(n_gx * owned, count, cz), held(cx // WIN, count * WIN, cz),
@@ -1059,7 +1053,7 @@
                     held(cx // WIN, comps * cy, cz), held(2, cy, cz),
                     held(2, comps, cy, cz), held(comps, cy, cz), held(3, comps, cy, cz),
                     held(cz, cz), pltpu.VMEM((3 * cz, cz), jnp.bfloat16), held(2, cy, cz),
-                    sems((10,)), sems((1,)), sems((4,)), sems((2,)), sems((2, comps)), sems((4,)),
+                    sems((10,)), sems((1,)), sems((4,)), sems((2, comps)), sems((2, comps)), sems((4,)),
                 ],
             )(*operands)
             return pulled

time: 22.2 us -> 21.9 us (0.986)
  Pallas kernels: 21.3 us -> 21 us
    pallas_call x1, Pallas kernels: 21.3 us -> 21 us  [local(): call(functools.partial(pair_kernel, sizes), scratch_shapes=loaded + [held...]
where the time goes in v4:
time: 21.9 us; the launch traced here: 21.6 us
  Pallas kernels  21 us (96%)
  local copies, waits for them, and re-layouts  0.68 us (3%)
    pallas_call x1, Pallas kernels, local(): call(functools.partial(pair_kernel, sizes), scratch_shapes=loaded + [held...  21 us
    unnamed x1, local copies, waits for them, and re-layouts  0.68 us

profile of v4, /device:TPU:0, one launch (start us, length us, event | category | flops | bytes accessed | tf_op | source)
XLA Modules:
  0.0 21.6 jit_solution(5653552130763918033)
XLA Ops:
  0.0 21.0 %shard_map.91 = f32[3,16,8,128]{3,2,1,0:T(8,128)S(1)} custom-call(f32[3,16,8,128]{3,2,1,0:T(8,128)} %dir_hbm.1, bf16[2,3,16,8,128]{4,3,2,1,0:T(8,128)(2,1)} %base_hbm.1, f32[4,16,16]{2,1,0:T(8,128)} %bitcast.2, f32[16,16]{1,0:T(8,128)} %local_h.1, f32[2,16]{1,0:T(2,128)} %in_h.1, f32[2,16]{1,0:T(2,128)} %bitcast.3, f32[4,4]{1,0:T(4,128)} %schur_h.1, ...), custom_call_target="tpu_custom_call" | custom-call | tf_op jit(solution)/shard_map/pallas_call | solution.py:1041
  21.0 0.7 %copy.11 = f32[3,16,8,128]{3,2,1,0:T(8,128)} copy(f32[3,16,8,128]{3,2,1,0:T(8,128)S(1)} %shard_map.91) | data formatting | bytes 393216

commit v5 on v4

--- a/solution.py
+++ b/solution.py
@@ -855,8 +855,8 @@
                 zsend[1, c] = packed(rows_of(acc, c)) + uz_pack[0] * face[c]
                 if c == comps - 1:
                     start(z_copies(1))
+                send_sides(1, c, acc)
                 send_y(1, c, acc)
-                send_sides(1, c, acc)
         closing = close(face)
         if r:
             uz_both.wait_recv()
@@ -916,14 +916,14 @@
         finish_src()
         for c in range(comps):
             for i in range(cx):
-                prod[c, i] = vel[n, 1, i] * src[c, i]
-            send_y(r, c, prod)
-            for i in range(cx):
                 rhs[c, i] = vel[n, 0, i] * src[c, i]
             for k in range(2):
                 xsend[r, c, k] = weighted([(local_s[j, near_row + k], rhs[c, j]) for j in range(cx)])
                 xsend[r, c, 2 + k] = weighted([(out_s[k, j], rhs[c, j]) for j in range(cx)])
             x_copy(r, c).start()
+            for i in range(cx):
+                prod[c, i] = vel[n, 1, i] * src[c, i]
+            send_y(r, c, prod)
         shadow()
         face = lateral(edge)
         for i in range(cx):

time: 21.9 us -> 21.9 us (level)
  no operation moved by 1% of the time
where the time goes in v5:
time: 21.9 us; the launch traced here: 21.6 us
  Pallas kernels  20.9 us (95%)
  local copies, waits for them, and re-layouts  0.68 us (3%)
    pallas_call x1, Pallas kernels, local(): call(functools.partial(pair_kernel, sizes), scratch_shapes=loaded + [held...  20.9 us
    unnamed x1, local copies, waits for them, and re-layouts  0.68 us

profile of v5, /device:TPU:0, one launch (start us, length us, event | category | flops | bytes accessed | tf_op | source)
XLA Modules:
  0.0 21.6 jit_solution(13921083117784167171)
XLA Ops:
  0.0 20.9 %shard_map.91 = f32[3,16,8,128]{3,2,1,0:T(8,128)S(1)} custom-call(f32[3,16,8,128]{3,2,1,0:T(8,128)} %dir_hbm.1, bf16[2,3,16,8,128]{4,3,2,1,0:T(8,128)(2,1)} %base_hbm.1, f32[4,16,16]{2,1,0:T(8,128)} %bitcast.2, f32[16,16]{1,0:T(8,128)} %local_h.1, f32[2,16]{1,0:T(2,128)} %in_h.1, f32[2,16]{1,0:T(2,128)} %bitcast.3, f32[4,4]{1,0:T(4,128)} %schur_h.1, ...), custom_call_target="tpu_custom_call" | custom-call | tf_op jit(solution)/shard_map/pallas_call | solution.py:1041
  20.9 0.7 %copy.11 = f32[3,16,8,128]{3,2,1,0:T(8,128)} copy(f32[3,16,8,128]{3,2,1,0:T(8,128)S(1)} %shard_map.91) | data formatting | bytes 393216
